TPU v7x, 256 devices: a whole 4x4x8 slice. The times are simulated.
256 devices in a mesh: date: 32 (over x, y, core), tile: 8 (over z).
Axes of the slice: x: 4, y: 4, z: 8, core: 2. Of those that a mesh axis runs over, the one named last changes fastest.
Arguments:
- slc: bfloat16 [2, 256, 10, 20480], P(None, 'date', None, 'tile'), may hold values from -3 to 3
- offsets: int32 [256, 20], replicated, may hold values from 0 to 24, as said below
Outputs:
- series: float32 [256, 8, 256], P(None, 'tile', 'date')
Inputs may be any that keep to these rules, and one draw needn't show every extreme that they name: In row d the live entries come first, are distinct, and satisfy d + offsets[d, k] <= 255; row d has min(c, 255 - d, 24) live entries with c from 4 to 20; the 8 rows of one index of date hold at most 100 live entries together, exactly 100 on some index; the remaining entries are 0.
All inputs are finite; a program needn't handle non-finite values.
Results may differ from a plain program's by a relative error of at most 0.0003.
Values may be sent and summed in bfloat16 or wider, within the bound.
A program may use at most 64 MiB of HBM per device.

v0:
```python
import jax
import jax.numpy as jnp
from jax import lax
from jax.sharding import PartitionSpec as P

LOOK_AZ = 5
LOOK_RG = 20
MAXP = 20
SPAN = 24
ITERS = 2


floor_value = 0.05
ridge_weight = 1.0
group_slots = 10


def shifted(block, axis, distance):
    devices = range(lax.axis_size(axis))
    route = [(i - distance, i) for i in devices if i - distance in devices]
    return lax.ppermute(block, axis, route)


def broadcast(block, axis, owner):
    block = jnp.where(lax.axis_index(axis) == owner, block, jnp.zeros_like(block))
    return lax.psum(block, axis)


def look_sums(first_rows, second_rows):
    first_real = first_rows[0].astype(jnp.float32)
    first_imag = first_rows[1].astype(jnp.float32)
    second_real = second_rows[0].astype(jnp.float32)
    second_imag = second_rows[1].astype(jnp.float32)
    real_part = first_real * second_real + first_imag * second_imag
    imag_part = first_imag * second_real - first_real * second_imag
    slot_count = real_part.shape[0]
    height = real_part.shape[1]
    tile_width = real_part.shape[2]
    shape_six = (slot_count, height // LOOK_AZ, LOOK_AZ, tile_width // LOOK_RG, LOOK_RG)
    real_looks = jnp.sum(real_part.reshape(shape_six), axis=(2, 4)).reshape(slot_count, -1)
    imag_looks = jnp.sum(imag_part.reshape(shape_six), axis=(2, 4)).reshape(slot_count, -1)
    return (real_looks, imag_looks)


def reweighted(phases, offsets):
    date_count = offsets.shape[0]
    is_live = offsets > 0
    second_date = jnp.arange(date_count, dtype=jnp.int32)[:, None] + offsets
    select = (
        (second_date[:, :, None] == jnp.arange(date_count, dtype=jnp.int32)[None, None, :])
        & is_live[:, :, None]
    ).astype(jnp.float32)
    live_weight = is_live.astype(jnp.float32)[:, :, None]
    pixels = phases.shape[2]
    series = jnp.zeros((date_count, pixels), jnp.float32)
    identity = jnp.eye(date_count, dtype=jnp.float32)
    highest = lax.Precision.HIGHEST
    for round_index in range(ITERS):
        later_values = jnp.einsum("dke,ep->dkp", select, series, precision=highest)
        residual = phases - (series[:, None, :] - later_values)
        weight = live_weight / jnp.maximum(jnp.abs(residual), floor_value)
        upper_band = jnp.einsum("dkp,dke->pde", weight, select, precision=highest)
        degree = jnp.sum(weight, axis=1).T + jnp.sum(upper_band, axis=1)
        gram_matrix = (
            ridge_weight * identity[None]
            + degree[:, :, None] * identity[None]
            - upper_band
            - jnp.swapaxes(upper_band, 1, 2)
        )
        weighted = weight * phases
        right_side = jnp.sum(weighted, axis=1) - jnp.einsum(
            "dkp,dke->ep", weighted, select, precision=highest
        )
        factor = jnp.linalg.cholesky(gram_matrix)
        middle = jax.scipy.linalg.solve_triangular(factor, right_side.T[:, :, None], lower=True)
        answer = jax.scipy.linalg.solve_triangular(factor, middle, lower=True, trans=1)
        series = answer[:, :, 0].T
    return series


def grouped_looks(window, first_index, second_index):
    slot_count = first_index.shape[0]
    group_count = slot_count // group_slots

    def one_group(members):
        first_rows = jnp.take(window, members[0], axis=1)
        second_rows = jnp.take(window, members[1], axis=1)
        return look_sums(first_rows, second_rows)

    real_looks, imag_looks = lax.map(
        one_group,
        (
            first_index.reshape(group_count, group_slots),
            second_index.reshape(group_count, group_slots),
        ),
    )
    return (real_looks.reshape(slot_count, -1), imag_looks.reshape(slot_count, -1))


def local(slc, offsets):
    date_local = slc.shape[1]
    date_count = offsets.shape[0]
    date_total = lax.axis_size("date")
    position = lax.axis_index("date")
    hop_total = (SPAN + date_local - 1) // date_local
    local_offsets = lax.dynamic_slice_in_dim(offsets, position * date_local, date_local, 0).reshape(
        -1
    )
    slot_ids = jnp.arange(local_offsets.shape[0], dtype=jnp.int32)
    slot_count = slot_ids.shape[0]
    received = [slc]
    for hop_index in range(1, hop_total + 1):
        received.append(shifted(slc, "date", -hop_index))
    extended = jnp.concatenate(received, axis=1)
    first_dates = slot_ids // MAXP
    second_dates = first_dates + jnp.take(local_offsets, slot_ids)
    real_looks, imag_looks = grouped_looks(extended, first_dates, second_dates)
    totals = jnp.stack([jnp.sum(real_looks, axis=1), jnp.sum(imag_looks, axis=1)])
    anchor = broadcast(totals, "tile", lax.axis_size("tile") // 2)
    phases = jnp.arctan2(imag_looks, real_looks) - jnp.arctan2(anchor[1], anchor[0])[:, None]
    owned_pixels = phases.shape[1] // date_total
    sectioned = phases.reshape(slot_count, date_total, owned_pixels)
    arrived = lax.all_to_all(sectioned, "date", split_axis=1, concat_axis=0, tiled=True)
    arrived_rows = arrived[:, 0, :]
    series = reweighted(arrived_rows.reshape(date_count, MAXP, -1), offsets)
    return series[:, None, :]


def solution(mesh):
    return jax.shard_map(
        local,
        mesh=mesh,
        in_specs=(P(None, "date", None, "tile"), P()),
        out_specs=P(None, "tile", "date"),
        check_vma=False,
    )
```

profile of v0, /device:TPU:1, one launch (start us, length us, event | category | flops | bytes accessed | tf_op | source)
XLA Modules:
  0.0 1624.8 jit_solution(13118934760318955091)
XLA Ops:
  16.0 12.7 collective-permute-done
  41.1 567.7 %while.20 = (s32[]{:T(128)}, f32[16,10,256]{2,1,0:T(8,128)}, f32[16,10,256]{2,1,0:T(8,128)}, s32[16,10]{1,0:T(8,128)S(1)}, bf16[2,32,10,2560]{3,2,1,0:T(8,128)(2...) while((s32[]{:T(128)}, f32[16,10,256]{2,1,0:T(8,128)}, f32[16,10,256]{2,1,0:T(8,128)}, ...), condition=%wide.region_3.5_spmd, body=%wide.region_0.4_spmd.sunk | while | flops 4093050 | bytes 18556360 | solution.py:90
  49.7 9.5 sub.135
  63.2 9.3 add.140
  85.2 9.5 sub.135
  98.7 9.3 add.140
  120.7 9.5 sub.135
  134.2 9.3 add.140
  156.1 9.5 sub.135
  169.7 9.3 add.140
  191.6 9.5 sub.135
  227.1 9.5 sub.135
  262.6 9.5 sub.135
  298.1 9.5 sub.135
  333.5 9.5 sub.135
  369.0 9.5 sub.135
  404.5 9.5 sub.135
  440.0 9.5 sub.135
  475.5 9.5 sub.135
  511.0 9.5 sub.135
  546.5 9.5 sub.135
  581.9 9.5 sub.135
  610.5 14.5 psum.7
  628.2 33.8 %all-to-all-start = ((f32[160,32,8]{0,2,1:T(8,128)}), f32[160,32,8]{0,2,1:T(8,128)S(1)}, u32[]{:S(2)}, u32[]{:S(2)}) async-start(f32[160,32,8]{0,2,1:T(8,128)} %broadcast_subtract_fusion), calls=%async_computation | async-start | bytes 524288 | tf_op jit(solution)/shard_map/all_to_all | solution.py:123
  693.0 94.4 %custom-call.21 = f32[8,128,128]{2,1,0:T(8,128)} custom-call(f32[8,128,128]{2,1,0:T(8,128)S(1)} %cholesky.198), custom_call_target="Cholesky" | custom-call | tf_op jit(solution)/shard_map/jit(cholesky)/cholesky | solution.py:74
  789.6 80.4 %custom-call.22 = f32[8,1,128,128]{2,3,1,0:T(8,128)} custom-call(f32[8,1,128,128]{3,2,1,0:T(8,128)} %select_bitcast_fusion.3), custom_call_target="InvertDiagBlocksLowerTriangular" | custom-call | tf_op jit(solution)/shard_map/jit(cholesky)/cholesky | solution.py:74
  874.9 95.2 %custom-call.23 = f32[8,128,128]{2,1,0:T(8,128)} custom-call(f32[8,128,128]{2,1,0:T(8,128)} %convolution_subtract_fusion.1), custom_call_target="Cholesky" | custom-call | tf_op jit(solution)/shard_map/jit(cholesky)/cholesky | solution.py:74
  981.8 158.8 %custom-call.25 = f32[8,2,128,128]{2,3,1,0:T(8,128)} custom-call(f32[8,2,128,128]{3,2,1,0:T(8,128)} %bitcast.253), custom_call_target="InvertDiagBlocksLowerTriangular" | custom-call | tf_op jit(solution)/shard_map/jit(_solve_triangular)/vmap()/triangular_solve | solution.py:76
  1168.1 94.0 %custom-call.26 = f32[8,128,128]{2,1,0:T(8,128)S(1)} custom-call(f32[8,128,128]{2,1,0:T(8,128)S(1)} %cholesky.201), custom_call_target="Cholesky" | custom-call | tf_op jit(solution)/shard_map/jit(cholesky)/cholesky | solution.py:74
  1265.0 80.0 %custom-call.27 = f32[8,1,128,128]{2,3,1,0:T(8,128)} custom-call(f32[8,1,128,128]{3,2,1,0:T(8,128)} %select_bitcast_fusion.2), custom_call_target="InvertDiagBlocksLowerTriangular" | custom-call | tf_op jit(solution)/shard_map/jit(cholesky)/cholesky | solution.py:74
  1349.9 95.2 %custom-call.28 = f32[8,128,128]{2,1,0:T(8,128)} custom-call(f32[8,128,128]{2,1,0:T(8,128)} %convolution_subtract_fusion), custom_call_target="Cholesky" | custom-call | tf_op jit(solution)/shard_map/jit(cholesky)/cholesky | solution.py:74
  1457.1 158.7 %custom-call.30 = f32[8,2,128,128]{2,3,1,0:T(8,128)} custom-call(f32[8,2,128,128]{3,2,1,0:T(8,128)} %bitcast.252), custom_call_target="InvertDiagBlocksLowerTriangular" | custom-call | tf_op jit(solution)/shard_map/jit(_solve_triangular)/vmap()/triangular_solve | solution.py:76
  (386 shorter events, 527.0 us)
Async XLA Ops:
  0.0 36.4 %copy-start.17 = (bf16[2,8,10,2560]{3,1,2,0:T(8,128)(2,1)S(1)}, bf16[2,8,10,2560]{3,1,2,0:T(8,128)(2,1)}, u32[]{:S(2)}) copy-start(bf16[2,8,10,2560]{3,1,2,0:T(8,128)(2,1)} %param.11) | copy-start | bytes 2457604
  0.0 28.7 %collective-permute-start = (bf16[2,8,10,2560]{3,1,2,0:T(8,128)(2,1)}, bf16[2,8,10,2560]{3,1,2,0:T(8,128)(2,1)S(1)}, u32[]{:S(2)}, u32[]{:S(2)}) collective-permute-start(bf16[2,8,10,2560]{3,1,2,0:T(8,128)(2,1)} %param.11), channel_id=1, source_target_pairs={{8,0},{16,8},{24,16},{32,24},{40,32},{48,40},{56,48},{64,56},{72,6... | collective-permute-start | bytes 2457608 | tf_op jit(solution)/shard_map/ppermute | solution.py:21
  5.2 31.1 %collective-permute-start.1 = (bf16[2,8,10,2560]{3,1,2,0:T(8,128)(2,1)}, bf16[2,8,10,2560]{3,1,2,0:T(8,128)(2,1)S(1)}, u32[]{:S(2)}, u32[]{:S(2)}) collective-permute-start(bf16[2,8,10,2560]{3,1,2,0:T(8,128)(2,1)} %param.11), channel_id=1, source_target_pairs={{16,0},{24,8},{32,16},{40,24},{48,32},{56,40},{64,48},{72,56},{80,... | collective-permute-start | bytes 2457608 | tf_op jit(solution)/shard_map/ppermute | solution.py:21
  6.5 29.8 %collective-permute-start.2 = (bf16[2,8,10,2560]{3,1,2,0:T(8,128)(2,1)}, bf16[2,8,10,2560]{3,1,2,0:T(8,128)(2,1)S(1)}, u32[]{:S(2)}, u32[]{:S(2)}) collective-permute-start(bf16[2,8,10,2560]{3,1,2,0:T(8,128)(2,1)} %param.11), channel_id=1, source_target_pairs={{24,0},{32,8},{40,16},{48,24},{56,32},{64,40},{72,48},{80,56},{88,... | collective-permute-start | bytes 2457608 | tf_op jit(solution)/shard_map/ppermute | solution.py:21
  627.5 44.2 %copy-start = (pred[256,20,256]{2,0,1:T(32,128)(4,1)S(1)}, pred[256,20,256]{2,0,1:T(32,128)(4,1)}, u32[]{:S(2)}) copy-start(pred[256,20,256]{2,0,1:T(32,128)(4,1)} %fusion.8) | copy-start | bytes 3932164
  628.2 42.7 %all-to-all-start = ((f32[160,32,8]{0,2,1:T(8,128)}), f32[160,32,8]{0,2,1:T(8,128)S(1)}, u32[]{:S(2)}, u32[]{:S(2)}) async-start(f32[160,32,8]{0,2,1:T(8,128)} %broadcast_subtract_fusion), calls=%async_computation | async-start | bytes 524288 | tf_op jit(solution)/shard_map/all_to_all | solution.py:123
  671.7 3.6 copy-start.13
  673.8 1.4 copy-start.16
  683.1 1.3 copy-start.2
  683.1 2.3 copy-start.4
  691.6 1.4 copy-start.8
  787.4 1.3 copy-start.10
  971.5 1.4 copy-start.5
  1140.6 5.1 copy-start.12
  1140.6 8.1 copy-start.14
  1150.8 0.7 copy-start.15
  1158.2 1.4 copy-start.1
  1158.2 2.3 copy-start.3
  1166.7 1.4 copy-start.7
  1262.1 0.8 copy-start.9
  1446.5 1.4 copy-start.6
  1615.7 5.0 copy-start.11
where the time goes:
time: 1640 us; the launch traced here: 1620 us
  other arithmetic  1030 us (63%)
  local copies, waits for them, and re-layouts  469 us (29%)
  starting transfers between devices  41.6 us (3%)
  matrix products  40.9 us (2%)
  waiting for transfers between devices  28.5 us (2%)
    another operation x18, other arithmetic, reweighted(): factor = jnp.linalg.cholesky(gram_matrix)  544 us
    another operation x8, other arithmetic, reweighted(): jax.scipy.linalg.solve_triangular(factor, middle, lower=True, trans=1)  321 us
    sub x16, local copies, waits for them, and re-layouts, look_sums(): imag_part = first_imag * second_real - first_real * second_imag  153 us
    add x16, local copies, waits for them, and re-layouts, look_sums(): real_part = first_real * second_real + first_imag * second_imag  149 us
    reduce_sum x16, other arithmetic, look_sums(): jnp.sum(imag_part.reshape(shape_six), axis=(2, 4)).reshape(slot_count, -1)  54 us
    reduce_sum x16, other arithmetic, look_sums(): jnp.sum(real_part.reshape(shape_six), axis=(2, 4)).reshape(slot_count, -1)  54 us
    gather x16, local copies, waits for them, and re-layouts, one_group(): first_rows = jnp.take(window, members[0], axis=1)  50.2 us
    gather x16, local copies, waits for them, and re-layouts, one_group(): second_rows = jnp.take(window, members[1], axis=1)  50.2 us
  transfers between devices with their start and end apart: 4, of which 3 were waited for; matrix products, arithmetic and copies ran while one was open for 1% of the time, Pallas kernels for 0%

commit v1 on v0

v1 whole, which is shorter than its diff:
```python
import jax
import jax.numpy as jnp
from jax import lax
from jax.experimental import pallas as pl
from jax.experimental.pallas import tpu as pltpu
from jax.sharding import PartitionSpec as P

LOOK_AZ = 5
LOOK_RG = 20
SPAN = 24
ITERS = 2
LANES = 128
WIN = 32

floor_value = 0.05
ridge_weight = 1.0
F32 = jnp.float32


def gather_kernel(slc_ref, out_ref, rows_ref):
    tiles = slc_ref.shape[3] // LANES
    for part in range(2):
        for date in range(8):
            base = (part * 8 + date) * 16
            block = slc_ref[part, date].astype(F32)
            for t in range(tiles):
                rows_ref[t, base:base + 10, :] = block[:, t * LANES:(t + 1) * LANES]
    lane = lax.broadcasted_iota(jnp.int32, (16, LANES), 1)

    def body(step, carry):
        half = step // 4
        quarter = step % 4
        shifted = []
        for rho in range(5):
            line = []
            for t in range(5):
                tile = quarter * 5 + t
                row = half * 5 + rho
                line.append(jnp.concatenate([
                    rows_ref[tile, pl.ds(row, 8, stride=16), :],
                    rows_ref[tile, pl.ds(128 + row, 8, stride=16), :],
                ], axis=0))
            shifted.append(line)
        moved = []
        for rho in range(5):
            amount = 20 * rho
            if amount == 0:
                moved.append(shifted[rho] + [jnp.zeros((16, LANES), F32)])
                continue
            rolled = [pltpu.roll(v, amount, 1) for v in shifted[rho]]
            line = []
            for t in range(6):
                left = rolled[t - 1] if t > 0 else jnp.zeros((16, LANES), F32)
                right = rolled[t] if t < 5 else jnp.zeros((16, LANES), F32)
                line.append(jnp.where(lane < amount, left, right))
            moved.append(line)
        for local_pixel in range(32):
            start = 20 * local_pixel
            tile, offset = start // LANES, start % LANES
            out = jnp.zeros((16, LANES), F32)
            for rho in range(5):
                lo = offset + 20 * rho
                hi = lo + 20
                if lo < LANES:
                    mask = (lane >= lo) & (lane < hi)
                    out = jnp.where(mask, moved[rho][tile], out)
                if hi > LANES:
                    mask = (lane >= lo - LANES) & (lane < hi - LANES)
                    out = jnp.where(mask, moved[rho][tile + 1], out)
            slot = half * 16 + quarter * 4 + local_pixel // 8
            out_ref[slot, local_pixel % 8] = out.astype(jnp.bfloat16)
        return carry

    lax.fori_loop(0, 8, body, 0)


def gather_samples(slc):
    cols = slc.shape[3]
    groups = 2 * cols // (8 * LOOK_RG)
    return pl.pallas_call(
        gather_kernel,
        out_shape=jax.ShapeDtypeStruct((groups, 8, 16, LANES), jnp.bfloat16),
        in_specs=[pl.BlockSpec(memory_space=pltpu.VMEM)],
        out_specs=pl.BlockSpec(memory_space=pltpu.VMEM),
        scratch_shapes=[pltpu.VMEM((cols // LANES, 256, LANES), F32)],
        name="gather_samples",
    )(slc)


def looks_kernel(samples_ref, looks_ref, anchor_ref, band_ref):
    lane = lax.broadcasted_iota(jnp.int32, (8, LANES), 1)
    contract = (((1,), (1,)), ((), ()))
    row_id = lax.broadcasted_iota(jnp.int32, (256, 256), 0)
    col_id = lax.broadcasted_iota(jnp.int32, (256, 256), 1)
    mirror = (row_id + col_id == 255).astype(F32).astype(jnp.bfloat16)
    for pixel in range(8):
        both = samples_ref[:, pixel].astype(F32)
        real = both[:, :8].reshape(256, LANES)
        imag = both[:, 8:].reshape(256, LANES)
        right = jnp.concatenate([real, imag], axis=1).astype(jnp.bfloat16)
        turned = jnp.concatenate([imag, -real], axis=1).astype(jnp.bfloat16)
        descending = jnp.dot(mirror, right, preferred_element_type=F32).astype(jnp.bfloat16)
        group, place = pixel // 4, pixel % 4
        inside = (lane >= place * WIN) & (lane < (place + 1) * WIN)
        for part, left in enumerate((right, turned)):
            gram = lax.dot_general(left, descending, contract, preferred_element_type=F32)
            for block in range(32):
                rows = gram[block * 8:block * 8 + 8, :]
                shift = (block * 8 + place * WIN + WIN) % 256
                skew = pltpu.roll(rows, shift, 1, stride=1, stride_axis=0)[:, :LANES]
                where = (part, group, pl.ds(block * 8, 8))
                if place == 0:
                    band_ref[where] = skew
                else:
                    band_ref[where] = jnp.where(inside, skew, band_ref[where])
    for part in range(2):
        for half in range(2):
            total = jnp.zeros((WIN, LANES), F32)
            for group in range(2):
                turned = band_ref[part, group, half * LANES:(half + 1) * LANES, :].T
                looks_ref[part, half, group * LANES:(group + 1) * LANES, :] = turned
                for place in range(4):
                    total = total + turned[place * WIN:(place + 1) * WIN]
            anchor_ref[part, half] = total


def pair_looks(samples):
    return pl.pallas_call(
        looks_kernel,
        out_shape=(
            jax.ShapeDtypeStruct((2, 2, 256, LANES), F32),
            jax.ShapeDtypeStruct((2, 2, WIN, LANES), F32),
        ),
        in_specs=[pl.BlockSpec(memory_space=pltpu.VMEM)],
        out_specs=(pl.BlockSpec(memory_space=pltpu.VMEM), pl.BlockSpec(memory_space=pltpu.VMEM)),
        scratch_shapes=[pltpu.VMEM((2, 2, 256, LANES), F32)],
        name="pair_looks",
    )(samples)


def factor_step(block, mat_ref, rhs_ref, low_ref, sol_ref):
    base = pl.multiple_of(block * 256, 256)

    def spread(ref, row):
        return jnp.broadcast_to(ref[pl.ds(row, 1), :], (8, LANES))

    s = {}
    for i in range(8):
        for j in range(i, 8):
            s[i, j] = spread(mat_ref, base + i * WIN + j)
    rows = []
    for i in range(8):
        tiles = [mat_ref[pl.ds(pl.multiple_of(base + i * WIN + 8 * t, 8), 8), :] for t in (1, 2, 3)]
        rows.append(tiles + [spread(rhs_ref, block * 8 + i)])
    mult = {}
    inverse = []
    for a in (0, 2, 4, 6):
        b = a + 1
        det = s[a, a] * s[b, b] - s[a, b] * s[a, b]
        scale = 1.0 / det
        e11, e12, e22 = s[b, b] * scale, -s[a, b] * scale, s[a, a] * scale
        inverse.append((e11, e12, e22))
        for i in range(a + 2, 8):
            mult[i, a] = s[a, i] * e11 + s[b, i] * e12
            mult[i, b] = s[a, i] * e12 + s[b, i] * e22
        for i in range(a + 2, 8):
            for j in range(i, 8):
                s[i, j] = s[i, j] - mult[i, a] * s[a, j] - mult[i, b] * s[b, j]
        for i in range(a + 2, 8):
            rows[i] = [rows[i][t] - mult[i, a] * rows[a][t] - mult[i, b] * rows[b][t] for t in range(4)]
    scaled = [None] * 8
    for index, a in enumerate((0, 2, 4, 6)):
        e11, e12, e22 = inverse[index]
        scaled[a] = [e11 * rows[a][t] + e12 * rows[a + 1][t] for t in range(4)]
        scaled[a + 1] = [e12 * rows[a][t] + e22 * rows[a + 1][t] for t in range(4)]
    for k in range(8):
        for t in range(3):
            low_ref[k * 24 + 8 * t:k * 24 + 8 * t + 8, :] = scaled[k][t]
    for r in range(24):
        t = r // 8
        target = pl.multiple_of((block + 1) * 256, 256) + r * WIN
        factors = [jnp.broadcast_to(low_ref[k * 24 + r:k * 24 + r + 1, :], (8, LANES)) for k in range(8)]
        for u in range(t, 3):
            where = pl.ds(pl.multiple_of(target + (u - t) * 8, 8), 8)
            value = mat_ref[where, :]
            for k in range(8):
                value = value - factors[k] * rows[k][u]
            mat_ref[where, :] = value
    for u in range(3):
        where = pl.ds(pl.multiple_of((block + 1 + u) * 8, 8), 8)
        value = rhs_ref[where, :]
        for k in range(8):
            value = value - scaled[k][3] * rows[k][u]
        rhs_ref[where, :] = value
    for a in (6, 4, 2, 0):
        for c in (a, a + 1):
            for i in range(a + 2, 8):
                scaled[c] = [scaled[c][t] - mult[i, c] * scaled[i][t] for t in range(4)]
    sub = lax.broadcasted_iota(jnp.int32, (8, LANES), 0)
    answer = scaled[0][3]
    for i in range(1, 8):
        answer = jnp.where(sub == i, scaled[i][3], answer)
    sol_ref[pl.ds(pl.multiple_of(block * 8, 8), 8), :] = answer
    for i in range(8):
        for t in range(3):
            mat_ref[pl.ds(pl.multiple_of(base + i * WIN + 8 * (t + 1), 8), 8), :] = scaled[i][t]


def back_step(block, mat_ref, sol_ref):
    base = pl.multiple_of(block * 256, 256)
    here = pl.ds(pl.multiple_of(block * 8, 8), 8)
    value = sol_ref[here, :]
    parts = []
    for c in range(23, -1, -1):
        column = mat_ref[pl.ds(base + 8 + c, 8, stride=WIN), :]
        later = jnp.broadcast_to(sol_ref[pl.ds((block + 1) * 8 + c, 1), :], (8, LANES))
        parts.append(column * later)
    while len(parts) > 1:
        parts = [parts[i] + parts[i + 1] if i + 1 < len(parts) else parts[i]
                 for i in range(0, len(parts), 2)]
    sol_ref[here, :] = value - parts[0]


def solve_kernel(looks_ref, anchor_ref, live_ref, out_ref, phase_ref, mat_ref, rhs_ref, low_ref, sol_ref):
    lane = lax.broadcasted_iota(jnp.int32, (8, LANES), 1)
    for half in range(2):
        base = jnp.arctan2(anchor_ref[1, half, :SPAN + 8, :], anchor_ref[0, half, :SPAN + 8, :])
        for pixel in range(8):
            where = slice(pixel * WIN, pixel * WIN + WIN)
            angle = jnp.arctan2(looks_ref[1, half, where, :], looks_ref[0, half, where, :])
            phase_ref[half, where, :] = angle - base
    sol_ref[...] = jnp.zeros_like(sol_ref)
    rhs_ref[...] = jnp.zeros_like(rhs_ref)
    filler = jnp.zeros((LANES - 8, LANES), F32)

    def turned(value):
        return jnp.concatenate([value, filler], axis=0).T

    def round_body(_, carry):
        now = [sol_ref[h * LANES:(h + 1) * LANES, :].T[:8] for h in range(2)]
        degree = [jnp.full((8, LANES), ridge_weight, F32) for _ in range(2)]
        right = [jnp.zeros((8, LANES), F32) for _ in range(2)]

        def clear(i, c):
            mat_ref[pl.ds(pl.multiple_of(i * WIN + 24, 8), 8), :] = jnp.zeros((8, LANES), F32)
            return c

        lax.fori_loop(0, 256, clear, 0, unroll=8)

        def ahead(pair, shift):
            a, b = (pltpu.roll(v, LANES - shift, 1) for v in pair)
            keep = lane < LANES - shift
            return [jnp.where(keep, a, b), jnp.where(keep, b, a)]

        def behind(pair, shift):
            a, b = (pltpu.roll(v, shift, 1) for v in pair)
            keep = lane >= shift
            return [jnp.where(keep, a, b), jnp.where(keep, b, a)]

        for d in range(1, SPAN + 1):
            later = ahead(now, d)
            weights, moments = [], []
            for h in range(2):
                phase = phase_ref[h, pl.ds(WIN - 1 - d, 8, stride=WIN), :]
                residual = phase - (now[h] - later[h])
                live = jnp.broadcast_to(live_ref[h, WIN - 1 - d:WIN - d, :], (8, LANES))
                weight = live / jnp.maximum(jnp.abs(residual), floor_value)
                weights.append(weight)
                moments.append(weight * phase)
            from_w, from_m = behind(weights, d), behind(moments, d)
            for h in range(2):
                degree[h] = degree[h] + (weights[h] + from_w[h])
                right[h] = right[h] + (moments[h] - from_m[h])
                column = turned(-weights[h])
                for b in range(16):
                    mat_ref[pl.ds((h * 16 + b) * 256 + d, 8, stride=WIN + 1), :] = column[b * 8:b * 8 + 8]
        for h in range(2):
            column = turned(degree[h])
            for b in range(16):
                mat_ref[pl.ds((h * 16 + b) * 256, 8, stride=WIN + 1), :] = column[b * 8:b * 8 + 8]
            rhs_ref[h * LANES:(h + 1) * LANES, :] = turned(right[h])

        def forward(i, c):
            factor_step(i, mat_ref, rhs_ref, low_ref, sol_ref)
            return c

        lax.fori_loop(0, 32, forward, 0)

        def backward(i, c):
            back_step(31 - i, mat_ref, sol_ref)
            return c

        lax.fori_loop(0, 32, backward, 0)
        return carry

    lax.fori_loop(0, ITERS, round_body, 0)
    out_ref[...] = sol_ref[:256, :8]


def solve(looks, anchor, live):
    return pl.pallas_call(
        solve_kernel,
        out_shape=jax.ShapeDtypeStruct((256, 8), F32),
        in_specs=[pl.BlockSpec(memory_space=pltpu.VMEM)] * 3,
        out_specs=pl.BlockSpec(memory_space=pltpu.VMEM),
        scratch_shapes=[
            pltpu.VMEM((2, 256, LANES), F32),
            pltpu.VMEM((280 * WIN, LANES), F32),
            pltpu.VMEM((280, LANES), F32),
            pltpu.VMEM((8 * 24, LANES), F32),
            pltpu.VMEM((280, LANES), F32),
        ],
        name="solve",
    )(looks, anchor, live)


def live_mask(offsets):
    distance = (WIN - 1 - jnp.arange(WIN, dtype=jnp.int32))[:, None, None]
    hit = jnp.any((offsets[None] == distance) & (offsets[None] > 0), axis=2)
    return hit.astype(F32).reshape(WIN, 2, LANES).transpose(1, 0, 2)


def local(slc, offsets):
    live = live_mask(offsets)
    samples = gather_samples(slc)
    samples = lax.all_to_all(samples, "date", split_axis=0, concat_axis=0, tiled=True)
    looks, partial = pair_looks(samples)
    owner = lax.axis_index("tile") == lax.axis_size("tile") // 2
    anchor = lax.psum(jnp.where(owner, partial, 0.0), ("date", "tile"))
    series = solve(looks, anchor, live)
    return series[:, None, :]


def solution(mesh):
    return jax.shard_map(
        local,
        mesh=mesh,
        in_specs=(P(None, "date", None, "tile"), P()),
        out_specs=P(None, "tile", "date"),
        check_vma=False,
    )
```

time: 1640 us -> 323 us (0.20)
  other arithmetic: 1030 us -> 1.42 us
  local copies, waits for them, and re-layouts: 469 us -> 5.03 us
  waiting for transfers between devices: 28.5 us -> 258 us
  matrix products: 40.9 us -> 0 us
  Pallas kernels: 0 us -> 36.3 us
  starting transfers between devices: 41.6 us -> 8.75 us
    another operation x30 -> x0, other arithmetic: 866 us -> none  [the longest x18 544 us: reweighted(): factor = jnp.linalg.cholesky(gram_matrix)]
    psum x0 -> x1, waiting for transfers between devices: none -> 241 us  [local(): anchor = lax.psum(jnp.where(owner, partial, 0.0), ('date', 'tile'))]
    sub x18 -> x0, local copies, waits for them, and re-layouts: 156 us -> none  [the longest x16 153 us: look_sums(): imag_part = first_imag * second_real - first_real * second_imag]
    add x16 -> x0, local copies, waits for them, and re-layouts: 149 us -> none  [look_sums(): real_part = first_real * second_real + first_imag * second_imag]
    reduce_sum x35 -> x0, other arithmetic: 110 us -> none  [the longest x16 54 us: look_sums(): jnp.sum(imag_part.reshape(shape_six), axis=(2, 4)).reshape(slot_count, -1)]
    gather x34 -> x0, local copies, waits for them, and re-layouts: 102 us -> none  [the longest x16 50.2 us: one_group(): first_rows = jnp.take(window, members[0], axis=1)]
    pallas_call x0 -> x3, Pallas kernels: none -> 36.3 us  [the longest x1 27.8 us: solve(): pl.pallas_call(solve_kernel, out_shape=jax.ShapeDtypeStruct((256, 8), F32...]
    sub x19 -> x1, other arithmetic: 34.6 us -> 0.01 us  [live_mask(): distance = (WIN - 1 - jnp.arange(WIN, dtype=jnp.int32))[:, None, None]]
  transfers between devices with their start and end apart: 4 -> 2, of which waited for: 3 -> 2; matrix products, arithmetic and copies ran while one was open for 1% -> 0% of each run, Pallas kernels for 0% -> 0%
where the time goes in v1:
time: 323 us
  waiting for transfers between devices  258 us (80%)
  Pallas kernels  36.3 us (11%)
  between operations  13.4 us (4%)
  starting transfers between devices  8.75 us (3%)
  local copies, waits for them, and re-layouts  5.03 us (2%)
    psum x1, waiting for transfers between devices, local(): anchor = lax.psum(jnp.where(owner, partial, 0.0), ('date', 'tile'))  241 us
    pallas_call x1, Pallas kernels, solve(): pl.pallas_call(solve_kernel, out_shape=jax.ShapeDtypeStruct((256, 8), F32...  27.8 us
    all_to_all x1, waiting for transfers between devices, local(): lax.all_to_all(samples, 'date', split_axis=0, concat_axis=0, tiled=True)  16.7 us
    all_to_all x1, starting transfers between devices, local(): lax.all_to_all(samples, 'date', split_axis=0, concat_axis=0, tiled=True)  8.71 us
  transfers between devices with their start and end apart: 2, of which 2 were waited for; matrix products, arithmetic and copies ran while one was open for 0% of the time, Pallas kernels for 0%

profile of v1, /device:TPU:1, one launch (start us, length us, event | category | flops | bytes accessed | tf_op | source)
XLA Modules:
  0.0 323.0 jit_solution(1871937237249698933)
XLA Ops:
  6.5 2.5 copy.12.slc_ref
  9.0 3.8 %gather_samples.1 = bf16[32,8,16,128]{3,2,1,0:T(8,128)(2,1)} custom-call(bf16[2,8,10,2560]{3,2,1,0:T(8,128)(2,1)} %copy.12.slc_ref), custom_call_target="tpu_custom_call" | custom-call | tf_op jit(solution)/shard_map/gather_samples/pallas_call | solution.py:80
  12.9 0.0 copy-start.1
  12.9 8.7 %all-to-all-start = ((bf16[32,8,16,128]{3,2,1,0:T(8,128)(2,1)}), bf16[32,8,16,128]{3,2,1,0:T(8,128)(2,1)S(1)}, u32[]{:S(2)}, u32[]{:S(2)}) async-start(bf16[32,8,16,128]{3,2,1,0:T(8,128)(2,1)} %gather_samples.1), calls=%async_computation | async-start | bytes 2097152 | tf_op jit(solution)/shard_map/all_to_all | solution.py:326
  21.6 0.0 all-reduce.2.cloned.1.call-start
  21.7 0.0 copy-done.1
  21.7 0.2 and_reduce_fusion
  21.8 16.7 %all-to-all-done.samples_ref = bf16[32,8,16,128]{3,2,1,0:T(8,128)(2,1)S(1)} async-done(((bf16[32,8,16,128]{3,2,1,0:T(8,128)(2,1)}), bf16[32,8,16,128]{3,2,1,0:T(8,128)(2,1)S(1)}, u32[]{:S(2)}, u32[]{:S(2)}) %all-to-all-start) | async-done | bytes 1048608 | tf_op jit(solution)/shard_map/all_to_all | solution.py:326
  38.5 0.0 copy-start
  38.5 1.0 copy-done
  39.5 4.7 %pair_looks.1 = (f32[2,2,256,128]{3,2,1,0:T(8,128)}, f32[2,2,32,128]{3,2,1,0:T(8,128)}) custom-call(bf16[32,8,16,128]{3,2,1,0:T(8,128)(2,1)} %copy-done), custom_call_target="tpu_custom_call" | custom-call | tf_op jit(solution)/shard_map/pair_looks/pallas_call | solution.py:128
  44.2 0.6 broadcast_select_fusion
  44.8 0.0 all-reduce.2.cloned.1.call-update
  44.8 0.6 bitcast_bitcast_fusion.live_ref
  45.4 241.3 %all-reduce.2.cloned.1.call-done.anchor_ref = f32[2,2,32,128]{3,2,1,0:T(8,128)} async-done(((f32[2,2,32,128]{3,2,1,0:T(8,128)}), f32[2,2,32,128]{3,2,1,0:T(8,128)}) %all-reduce.2.cloned.1.call-update) | async-done | bytes 65552 | tf_op jit(solution)/shard_map/psum | solution.py:329
  286.7 27.8 %solve.1 = f32[256,8]{1,0:T(8,128)} custom-call(f32[2,2,256,128]{3,2,1,0:T(8,128)} %get-tuple-element.7.looks_ref, f32[2,2,32,128]{3,2,1,0:T(8,128)} %all-reduce.2.cloned.1.call-done.anchor_ref, f32[2,32,128]{2,1,0:T(8,128)} %bitcast_bitcast_fusion.live_ref), custom_call_target="tpu_custom_call" | custom-call | tf_op jit(solution)/shard_map/solve/pallas_call | solution.py:301
  314.5 1.6 copy.14
  (2 shorter events, 0.0 us)
Async XLA Ops:
  12.9 8.8 %copy-start.1 = (s32[256,20]{0,1:T(8,128)S(1)}, s32[256,20]{0,1:T(8,128)}, u32[]{:S(2)}) copy-start(s32[256,20]{0,1:T(8,128)} %param.3) | copy-start | bytes 61444
  12.9 25.6 %all-to-all-start = ((bf16[32,8,16,128]{3,2,1,0:T(8,128)(2,1)}), bf16[32,8,16,128]{3,2,1,0:T(8,128)(2,1)S(1)}, u32[]{:S(2)}, u32[]{:S(2)}) async-start(bf16[32,8,16,128]{3,2,1,0:T(8,128)(2,1)} %gather_samples.1), calls=%async_computation | async-start | bytes 2097152 | tf_op jit(solution)/shard_map/all_to_all | solution.py:326
  21.6 265.1 %all-reduce.2.cloned.1.call-start = ((), (), s32[]{:S(2)}) async-start(), calls=%async_computation.1 | async-start | bytes 131072 | tf_op jit(solution)/shard_map/psum | solution.py:329
  38.5 1.0 copy-start
Sparse Core Ops, SparseCore 0:
  44.9 241.7 all-reduce.1

commit v2 on v1

v2 whole, which is shorter than its diff:
```python
import jax
import jax.numpy as jnp
from jax import lax
from jax.experimental import pallas as pl
from jax.experimental.pallas import tpu as pltpu
from jax.sharding import PartitionSpec as P

LOOK_AZ = 5
LOOK_RG = 20
SPAN = 24
ITERS = 2
LANES = 128
WIN = 32

floor_value = 0.05
ridge_weight = 1.0
F32 = jnp.float32
MESH = pl.DeviceIdType.MESH
OWNERS = 6
OWNER_STEP = 5


def gather_step(step, slc_ref, send_ref):
    lane = lax.broadcasted_iota(jnp.int32, (16, LANES), 1)
    half = step // 4
    quarter = step % 4
    blank = jnp.zeros((16, LANES), F32)
    moved = []
    for rho in range(LOOK_AZ):
        amount = LOOK_RG * rho
        line = []
        for t in range(5):
            columns = pl.ds(pl.multiple_of((quarter * 5 + t) * LANES, LANES), LANES)
            row = half * LOOK_AZ + rho
            line.append(jnp.concatenate([
                slc_ref[0, row, :, columns].astype(F32),
                slc_ref[1, row, :, columns].astype(F32),
            ], axis=0))
        if amount == 0:
            moved.append(line + [blank])
            continue
        rolled = [blank] + [pltpu.roll(v, amount, 1) for v in line] + [blank]
        moved.append([jnp.where(lane < amount, rolled[t], rolled[t + 1]) for t in range(6)])
    for local_pixel in range(32):
        start = LOOK_RG * local_pixel
        tile, offset = start // LANES, start % LANES
        out = blank
        for rho in range(LOOK_AZ):
            lo = offset + LOOK_RG * rho
            hi = lo + LOOK_RG
            if lo < LANES:
                out = jnp.where((lane >= lo) & (lane < hi), moved[rho][tile], out)
            if hi > LANES:
                mask = (lane >= lo - LANES) & (lane < hi - LANES)
                out = jnp.where(mask, moved[rho][tile + 1], out)
        slot = half * 16 + quarter * 4 + local_pixel // 8
        send_ref[slot, local_pixel % 8] = out.astype(jnp.bfloat16)


def skewed(gram_ref, index, block, place):
    rows = pl.ds(block * 8, 8)
    first = gram_ref[index + (rows, pl.ds(0, LANES))] if block >= 13 else None
    second = gram_ref[index + (rows, pl.ds(LANES, LANES))] if block < 16 else None
    if first is None:
        value = second
    elif second is None:
        value = first
    else:
        lane = lax.broadcasted_iota(jnp.int32, (8, LANES), 1)
        value = jnp.where(lane >= 64, first, second)
    shift = (place * WIN + SPAN + 1 + block * 8) % LANES
    return pltpu.roll(value, shift, 1, stride=1, stride_axis=0)


def front_kernel(slc_ref, phase_ref, send_ref, recv_ref, gram_ref, total_ref, band_ref, part_ref,
                 gathered_ref, anchor_ref, send_sem, recv_sem, part_send, part_recv, column_send,
                 column_recv, plane_send, plane_recv):
    dates = send_ref.shape[0]
    tiles = lax.axis_size("tile")
    me = lax.axis_index("date")
    tile = lax.axis_index("tile")
    middle = tiles // 2
    lane = lax.broadcasted_iota(jnp.int32, (8, LANES), 1)

    def peer(k):
        return lax.rem(me + k, dates)

    barrier = pltpu.get_barrier_semaphore()

    def greet(k, carry):
        pl.semaphore_signal(barrier, inc=1, device_id={"date": peer(k)}, device_id_type=MESH)
        return carry

    def greet_column(k, carry):
        pl.semaphore_signal(barrier, inc=1, device_id={"tile": lax.rem(tile + k, tiles)}, device_id_type=MESH)
        return carry

    lax.fori_loop(1, dates, greet, 0)
    lax.fori_loop(1, tiles, greet_column, 0)

    def gather(step, carry):
        gather_step(step, slc_ref, send_ref)
        return carry

    lax.fori_loop(0, 8, gather, 0)
    pl.semaphore_wait(barrier, dates - 1 + tiles - 1)

    def sample_copy(other, slot):
        return pltpu.make_async_remote_copy(
            src_ref=send_ref.at[other], dst_ref=recv_ref.at[slot],
            send_sem=send_sem.at[other], recv_sem=recv_sem.at[slot],
            device_id={"date": other}, device_id_type=MESH)

    def send(k, carry):
        sample_copy(peer(k), me).start()
        return carry

    lax.fori_loop(1, dates, send, 0)
    recv_ref[me] = send_ref[me]

    def arrive(k, carry):
        other = peer(k)
        sample_copy(other, other).wait_recv()
        return carry

    lax.fori_loop(1, dates, arrive, 0)

    row_id = lax.broadcasted_iota(jnp.int32, (256, 256), 0)
    col_id = lax.broadcasted_iota(jnp.int32, (256, 256), 1)
    mirror = (row_id + col_id == 255).astype(F32).astype(jnp.bfloat16)
    contract = (((1,), (1,)), ((), ()))
    total_ref[...] = jnp.zeros_like(total_ref)

    def grams(pixel, carry):
        both = recv_ref[:, pixel].astype(F32)
        real = both[:, :8].reshape(256, LANES)
        imag = both[:, 8:].reshape(256, LANES)
        right = jnp.concatenate([real, imag], axis=1).astype(jnp.bfloat16)
        turned = jnp.concatenate([imag, -real], axis=1).astype(jnp.bfloat16)
        descending = jnp.dot(mirror, right, preferred_element_type=F32).astype(jnp.bfloat16)
        for part, left in enumerate((right, turned)):
            gram = lax.dot_general(left, descending, contract, preferred_element_type=F32)
            gram_ref[pixel, part] = gram
            total_ref[part] = total_ref[part] + gram
        return carry

    lax.fori_loop(0, 8, grams, 0)

    def part_copy(owner, slot):
        return pltpu.make_async_remote_copy(
            src_ref=part_ref.at[owner], dst_ref=gathered_ref.at[slot],
            send_sem=part_send.at[owner], recv_sem=part_recv.at[slot],
            device_id={"date": owner * OWNER_STEP}, device_id_type=MESH)

    @pl.when(tile == middle)
    def _():
        for block in range(32):
            value = jnp.where(lane < WIN, skewed(total_ref, (0,), block, 0), skewed(total_ref, (1,), block, 1))
            band_ref[0, 0, block * 8:block * 8 + 8, :] = value
        for half in range(2):
            turned = band_ref[0, 0, half * LANES:(half + 1) * LANES, :].T
            for third in range(3):
                owner = half * 3 + third
                part_ref[owner, 0:8, :] = turned[third * 8:third * 8 + 8]
                part_ref[owner, 8:16, :] = turned[WIN + third * 8:WIN + third * 8 + 8]
        for owner in range(OWNERS):
            @pl.when(me != owner * OWNER_STEP)
            def _():
                part_copy(owner, me).start()

    def bands(group, carry):
        for part in range(2):
            for block in range(32):
                value = skewed(gram_ref, (group * 4, part), block, 0)
                for place in range(1, 4):
                    other = skewed(gram_ref, (group * 4 + place, part), block, place)
                    value = jnp.where(lane < place * WIN, value, other)
                band_ref[part, group, block * 8:block * 8 + 8, :] = value
        for half in range(2):
            rows = slice(half * LANES, (half + 1) * LANES)
            real = band_ref[0, group, rows, :].T
            imag = band_ref[1, group, rows, :].T
            phase_ref[half, pl.ds(pl.multiple_of(group * LANES, LANES), LANES), :] = jnp.arctan2(imag, real)
        return carry

    lax.fori_loop(0, 2, bands, 0)

    def column_copy(owner, other):
        return pltpu.make_async_remote_copy(
            src_ref=anchor_ref.at[owner], dst_ref=anchor_ref.at[owner],
            send_sem=column_send.at[other], recv_sem=column_recv.at[0],
            device_id={"tile": other}, device_id_type=MESH)

    def plane_copy(owner, other):
        return pltpu.make_async_remote_copy(
            src_ref=anchor_ref.at[owner], dst_ref=anchor_ref.at[owner],
            send_sem=plane_send.at[other], recv_sem=plane_recv.at[owner],
            device_id={"date": other}, device_id_type=MESH)

    def plane_start(owner):
        def go(k, carry):
            plane_copy(owner, peer(k)).start()
            return carry

        lax.fori_loop(1, dates, go, 0)

    for owner in range(OWNERS):
        @pl.when((me == owner * OWNER_STEP) & (tile == middle))
        def _():
            def part_arrive(k, total):
                other = peer(k)
                part_copy(owner, other).wait_recv()
                return total + gathered_ref[other]

            total = lax.fori_loop(1, dates, part_arrive, part_ref[owner])
            anchor_ref[owner] = jnp.arctan2(total[8:], total[:8])

            def go(k, carry):
                column_copy(owner, lax.rem(tile + k, tiles)).start()
                return carry

            lax.fori_loop(1, tiles, go, 0)
            plane_start(owner)

        @pl.when((me == owner * OWNER_STEP) & (tile != middle))
        def _():
            column_copy(owner, middle).wait_recv()
            plane_start(owner)

    for owner in range(OWNERS):
        @pl.when(me != owner * OWNER_STEP)
        def _():
            plane_copy(owner, owner * OWNER_STEP).wait_recv()

    for half in range(2):
        base = jnp.concatenate([anchor_ref[half * 3 + t] for t in range(3)], axis=0)
        for pixel in range(8):
            rows = slice(pixel * WIN, pixel * WIN + SPAN)
            phase_ref[half, rows, :] = phase_ref[half, rows, :] - base

    def drain(k, carry):
        sample_copy(peer(k), me).wait_send()
        return carry

    lax.fori_loop(1, dates, drain, 0)
    for owner in range(OWNERS):
        @pl.when((me != owner * OWNER_STEP) & (tile == middle))
        def _():
            part_copy(owner, me).wait_send()

        @pl.when(me == owner * OWNER_STEP)
        def _():
            def done(k, carry):
                plane_copy(owner, peer(k)).wait_send()
                return carry

            lax.fori_loop(1, dates, done, 0)

        @pl.when((me == owner * OWNER_STEP) & (tile == middle))
        def _():
            def done(k, carry):
                column_copy(owner, lax.rem(tile + k, tiles)).wait_send()
                return carry

            lax.fori_loop(1, tiles, done, 0)


def pair_phases(slc, dates, tiles):
    groups = dates
    return pl.pallas_call(
        front_kernel,
        out_shape=jax.ShapeDtypeStruct((2, 256, LANES), F32),
        in_specs=[pl.BlockSpec(memory_space=pltpu.VMEM)],
        out_specs=pl.BlockSpec(memory_space=pltpu.VMEM),
        scratch_shapes=[
            pltpu.VMEM((groups, 8, 16, LANES), jnp.bfloat16),
            pltpu.VMEM((groups, 8, 16, LANES), jnp.bfloat16),
            pltpu.VMEM((8, 2, 256, 256), F32),
            pltpu.VMEM((2, 256, 256), F32),
            pltpu.VMEM((2, 2, 256, LANES), F32),
            pltpu.VMEM((OWNERS, 16, LANES), F32),
            pltpu.VMEM((groups, 16, LANES), F32),
            pltpu.VMEM((OWNERS, 8, LANES), F32),
            pltpu.SemaphoreType.DMA((groups,)),
            pltpu.SemaphoreType.DMA((groups,)),
            pltpu.SemaphoreType.DMA((OWNERS,)),
            pltpu.SemaphoreType.DMA((groups,)),
            pltpu.SemaphoreType.DMA((tiles,)),
            pltpu.SemaphoreType.DMA((1,)),
            pltpu.SemaphoreType.DMA((groups,)),
            pltpu.SemaphoreType.DMA((OWNERS,)),
        ],
        compiler_params=pltpu.CompilerParams(collective_id=0, has_side_effects=True),
        name="pair_phases",
    )(slc)


def factor_step(block, mat_ref, rhs_ref, low_ref, sol_ref):
    base = pl.multiple_of(block * 256, 256)

    def spread(ref, row):
        return jnp.broadcast_to(ref[pl.ds(row, 1), :], (8, LANES))

    s = {}
    for i in range(8):
        for j in range(i, 8):
            s[i, j] = spread(mat_ref, base + i * WIN + j)
    rows = []
    for i in range(8):
        tiles = [mat_ref[pl.ds(pl.multiple_of(base + i * WIN + 8 * t, 8), 8), :] for t in (1, 2, 3)]
        rows.append(tiles + [spread(rhs_ref, block * 8 + i)])
    mult = {}
    inverse = []
    for a in (0, 2, 4, 6):
        b = a + 1
        det = s[a, a] * s[b, b] - s[a, b] * s[a, b]
        scale = 1.0 / det
        e11, e12, e22 = s[b, b] * scale, -s[a, b] * scale, s[a, a] * scale
        inverse.append((e11, e12, e22))
        for i in range(a + 2, 8):
            mult[i, a] = s[a, i] * e11 + s[b, i] * e12
            mult[i, b] = s[a, i] * e12 + s[b, i] * e22
        for i in range(a + 2, 8):
            for j in range(i, 8):
                s[i, j] = s[i, j] - mult[i, a] * s[a, j] - mult[i, b] * s[b, j]
        for i in range(a + 2, 8):
            rows[i] = [rows[i][t] - mult[i, a] * rows[a][t] - mult[i, b] * rows[b][t] for t in range(4)]
    scaled = [None] * 8
    for index, a in enumerate((0, 2, 4, 6)):
        e11, e12, e22 = inverse[index]
        scaled[a] = [e11 * rows[a][t] + e12 * rows[a + 1][t] for t in range(4)]
        scaled[a + 1] = [e12 * rows[a][t] + e22 * rows[a + 1][t] for t in range(4)]
    for k in range(8):
        for t in range(3):
            low_ref[k * 24 + 8 * t:k * 24 + 8 * t + 8, :] = scaled[k][t]
    for r in range(24):
        t = r // 8
        target = pl.multiple_of((block + 1) * 256, 256) + r * WIN
        factors = [jnp.broadcast_to(low_ref[k * 24 + r:k * 24 + r + 1, :], (8, LANES)) for k in range(8)]
        for u in range(t, 3):
            where = pl.ds(pl.multiple_of(target + (u - t) * 8, 8), 8)
            value = mat_ref[where, :]
            for k in range(8):
                value = value - factors[k] * rows[k][u]
            mat_ref[where, :] = value
    for u in range(3):
        where = pl.ds(pl.multiple_of((block + 1 + u) * 8, 8), 8)
        value = rhs_ref[where, :]
        for k in range(8):
            value = value - scaled[k][3] * rows[k][u]
        rhs_ref[where, :] = value
    for a in (6, 4, 2, 0):
        for c in (a, a + 1):
            for i in range(a + 2, 8):
                scaled[c] = [scaled[c][t] - mult[i, c] * scaled[i][t] for t in range(4)]
    sub = lax.broadcasted_iota(jnp.int32, (8, LANES), 0)
    answer = scaled[0][3]
    for i in range(1, 8):
        answer = jnp.where(sub == i, scaled[i][3], answer)
    sol_ref[pl.ds(pl.multiple_of(block * 8, 8), 8), :] = answer
    for i in range(8):
        for t in range(3):
            mat_ref[pl.ds(pl.multiple_of(base + i * WIN + 8 * (t + 1), 8), 8), :] = scaled[i][t]


def back_step(block, mat_ref, sol_ref):
    base = pl.multiple_of(block * 256, 256)
    here = pl.ds(pl.multiple_of(block * 8, 8), 8)
    value = sol_ref[here, :]
    parts = []
    for c in range(23, -1, -1):
        column = mat_ref[pl.ds(base + 8 + c, 8, stride=WIN), :]
        later = jnp.broadcast_to(sol_ref[pl.ds((block + 1) * 8 + c, 1), :], (8, LANES))
        parts.append(column * later)
    while len(parts) > 1:
        parts = [parts[i] + parts[i + 1] if i + 1 < len(parts) else parts[i]
                 for i in range(0, len(parts), 2)]
    sol_ref[here, :] = value - parts[0]


def solve_kernel(phase_ref, live_ref, out_ref, mat_ref, rhs_ref, low_ref, sol_ref):
    lane = lax.broadcasted_iota(jnp.int32, (8, LANES), 1)
    sol_ref[...] = jnp.zeros_like(sol_ref)
    rhs_ref[...] = jnp.zeros_like(rhs_ref)
    filler = jnp.zeros((LANES - 8, LANES), F32)

    def turned(value):
        return jnp.concatenate([value, filler], axis=0).T

    def round_body(_, carry):
        now = [sol_ref[h * LANES:(h + 1) * LANES, :].T[:8] for h in range(2)]
        degree = [jnp.full((8, LANES), ridge_weight, F32) for _ in range(2)]
        right = [jnp.zeros((8, LANES), F32) for _ in range(2)]

        def clear(i, c):
            mat_ref[pl.ds(pl.multiple_of(i * WIN + 24, 8), 8), :] = jnp.zeros((8, LANES), F32)
            return c

        lax.fori_loop(0, 256, clear, 0, unroll=8)

        def ahead(pair, shift):
            a, b = (pltpu.roll(v, LANES - shift, 1) for v in pair)
            keep = lane < LANES - shift
            return [jnp.where(keep, a, b), jnp.where(keep, b, a)]

        def behind(pair, shift):
            a, b = (pltpu.roll(v, shift, 1) for v in pair)
            keep = lane >= shift
            return [jnp.where(keep, a, b), jnp.where(keep, b, a)]

        for d in range(1, SPAN + 1):
            later = ahead(now, d)
            weights, moments = [], []
            for h in range(2):
                phase = phase_ref[h, pl.ds(SPAN - d, 8, stride=WIN), :]
                residual = phase - (now[h] - later[h])
                live = jnp.broadcast_to(live_ref[h, SPAN - d:SPAN - d + 1, :], (8, LANES))
                weight = live / jnp.maximum(jnp.abs(residual), floor_value)
                weights.append(weight)
                moments.append(weight * phase)
            from_w, from_m = behind(weights, d), behind(moments, d)
            for h in range(2):
                degree[h] = degree[h] + (weights[h] + from_w[h])
                right[h] = right[h] + (moments[h] - from_m[h])
                column = turned(-weights[h])
                for b in range(16):
                    mat_ref[pl.ds((h * 16 + b) * 256 + d, 8, stride=WIN + 1), :] = column[b * 8:b * 8 + 8]
        for h in range(2):
            column = turned(degree[h])
            for b in range(16):
                mat_ref[pl.ds((h * 16 + b) * 256, 8, stride=WIN + 1), :] = column[b * 8:b * 8 + 8]
            rhs_ref[h * LANES:(h + 1) * LANES, :] = turned(right[h])

        def forward(i, c):
            factor_step(i, mat_ref, rhs_ref, low_ref, sol_ref)
            return c

        lax.fori_loop(0, 32, forward, 0)

        def backward(i, c):
            back_step(31 - i, mat_ref, sol_ref)
            return c

        lax.fori_loop(0, 32, backward, 0)
        return carry

    lax.fori_loop(0, ITERS, round_body, 0)
    for h in range(2):
        out_ref[:, h * LANES:(h + 1) * LANES] = sol_ref[h * LANES:(h + 1) * LANES, :].T[:8]


def solve(phases, live):
    return pl.pallas_call(
        solve_kernel,
        out_shape=jax.ShapeDtypeStruct((8, 256), F32),
        in_specs=[pl.BlockSpec(memory_space=pltpu.VMEM)] * 2,
        out_specs=pl.BlockSpec(memory_space=pltpu.VMEM),
        scratch_shapes=[
            pltpu.VMEM((280 * WIN, LANES), F32),
            pltpu.VMEM((280, LANES), F32),
            pltpu.VMEM((8 * 24, LANES), F32),
            pltpu.VMEM((280, LANES), F32),
        ],
        name="solve",
    )(phases, live)


def live_mask(offsets):
    distance = (SPAN - jnp.arange(WIN, dtype=jnp.int32))[:, None, None]
    hit = jnp.any((offsets[None] == distance) & (offsets[None] > 0), axis=2)
    return hit.astype(F32).reshape(WIN, 2, LANES).transpose(1, 0, 2)


def local(slc, offsets):
    live = live_mask(offsets)
    rows_first = jnp.transpose(slc, (0, 2, 1, 3))
    phases = pair_phases(rows_first, lax.axis_size("date"), lax.axis_size("tile"))
    series = solve(phases, live)
    return series.T[:, None, :]


def solution(mesh):
    return jax.shard_map(
        local,
        mesh=mesh,
        in_specs=(P(None, "date", None, "tile"), P()),
        out_specs=P(None, "tile", "date"),
        check_vma=False,
    )
```

time: 323 us -> 78.8 us (0.24)
  waiting for transfers between devices: 258 us -> 0 us
  Pallas kernels: 36.3 us -> 77 us
  between operations: 13.4 us -> 0.01 us
  starting transfers between devices: 8.75 us -> 0 us
  local copies, waits for them, and re-layouts: 5.03 us -> 0.01 us
    psum x1 -> x0, waiting for transfers between devices: 241 us -> none  [local(): anchor = lax.psum(jnp.where(owner, partial, 0.0), ('date', 'tile'))]
    pallas_call x3 -> x2, Pallas kernels: 36.3 us -> 77 us  [the longest x1 49.8 us: pair_phases(): pl.pallas_call(front_kernel, out_shape=jax.ShapeDtypeStruct((2, 256, LANE...]
    all_to_all x1 -> x0, waiting for transfers between devices: 16.7 us -> none  [local(): lax.all_to_all(samples, 'date', split_axis=0, concat_axis=0, tiled=True)]
    all_to_all x1 -> x0, starting transfers between devices: 8.71 us -> none  [local(): lax.all_to_all(samples, 'date', split_axis=0, concat_axis=0, tiled=True)]
    unnamed x5 -> x2, local copies, waits for them, and re-layouts: 3.46 us -> 0.01 us
  transfers between devices with their start and end apart: 2 -> 0, of which waited for: 2 -> 0; matrix products, arithmetic and copies ran while one was open for 0% -> 0% of each run, Pallas kernels for 0% -> 0%
where the time goes in v2:
time: 78.8 us; the launch traced here: 78.6 us
  Pallas kernels  77 us (98%)
  other arithmetic  1.59 us (2%)
    pallas_call x1, Pallas kernels, pair_phases(): pl.pallas_call(front_kernel, out_shape=jax.ShapeDtypeStruct((2, 256, LANE...  49.8 us
    pallas_call x1, Pallas kernels, solve(): pl.pallas_call(solve_kernel, out_shape=jax.ShapeDtypeStruct((8, 256), F32...  27.3 us

profile of v2, /device:TPU:1, one launch (start us, length us, event | category | flops | bytes accessed | tf_op | source)
XLA Modules:
  0.0 78.6 jit_solution(17315380486464041990)
XLA Ops:
  0.0 0.0 copy-start
  0.0 0.8 %broadcast_compare_fusion = pred[256,20]{0,1:T(8,128)(4,1)S(1)} fusion(s32[256,20]{0,1:T(8,128)} %param.3), kind=kLoop, calls=%fused_computation.3 | loop fusion | flops 5120 | bytes 25600 | tf_op jit(solution)/shard_map/gt | solution.py:470
  0.8 0.0 copy-done
  0.8 0.2 and_reduce_fusion
  1.0 0.6 bitcast_bitcast_fusion.live_ref
  1.6 49.8 %pair_phases.1.phase_ref = f32[2,256,128]{2,1,0:T(8,128)} custom-call(bf16[2,10,8,2560]{3,2,1,0:T(8,128)(2,1)} %bitcast.11), custom_call_target="tpu_custom_call" | custom-call | tf_op jit(solution)/shard_map/pair_phases/pallas_call | solution.py:270
  51.4 27.3 %solve.1 = f32[8,256]{1,0:T(8,128)} custom-call(f32[2,256,128]{2,1,0:T(8,128)} %pair_phases.1.phase_ref, f32[2,32,128]{2,1,0:T(8,128)} %bitcast_bitcast_fusion.live_ref), custom_call_target="tpu_custom_call" | custom-call | tf_op jit(solution)/shard_map/solve/pallas_call | solution.py:453
  (1 shorter events, 0.0 us)
Async XLA Ops:
  0.0 0.8 %copy-start = (s32[256,20]{0,1:T(8,128)S(1)}, s32[256,20]{0,1:T(8,128)}, u32[]{:S(2)}) copy-start(s32[256,20]{0,1:T(8,128)} %param.3) | copy-start | bytes 61444

commit v3 on v2

--- a/solution.py
+++ b/solution.py
@@ -295,7 +295,7 @@
     )(slc)
 
 
-def factor_step(block, mat_ref, rhs_ref, low_ref, sol_ref):
+def factor_step(block, mat_ref, rhs_ref, low_ref, back_ref, sol_ref):
     base = pl.multiple_of(block * 256, 256)
 
     def spread(ref, row):
@@ -360,54 +360,116 @@
     sol_ref[pl.ds(pl.multiple_of(block * 8, 8), 8), :] = answer
     for i in range(8):
         for t in range(3):
-            mat_ref[pl.ds(pl.multiple_of(base + i * WIN + 8 * (t + 1), 8), 8), :] = scaled[i][t]
-
-
-def back_step(block, mat_ref, sol_ref):
-    base = pl.multiple_of(block * 256, 256)
-    here = pl.ds(pl.multiple_of(block * 8, 8), 8)
-    value = sol_ref[here, :]
-    parts = []
-    for c in range(23, -1, -1):
-        column = mat_ref[pl.ds(base + 8 + c, 8, stride=WIN), :]
-        later = jnp.broadcast_to(sol_ref[pl.ds((block + 1) * 8 + c, 1), :], (8, LANES))
-        parts.append(column * later)
+            back_ref[pl.ds((block * 24 + 8 * t) * 9 + i, 8, stride=9), :] = scaled[i][t]
+
+
+def tree_sum(parts):
     while len(parts) > 1:
         parts = [parts[i] + parts[i + 1] if i + 1 < len(parts) else parts[i]
                  for i in range(0, len(parts), 2)]
-    sol_ref[here, :] = value - parts[0]
-
-
-def solve_kernel(phase_ref, live_ref, out_ref, mat_ref, rhs_ref, low_ref, sol_ref):
+    return parts[0]
+
+
+def back_step(block, back_ref, sol_ref):
+    rows = slice(block * 8, block * 8 + 8)
+
+    def product(c):
+        start = (block * 24 + c) * 9
+        later = jnp.broadcast_to(sol_ref[block * 8 + 8 + c:block * 8 + 9 + c, :], (8, LANES))
+        return back_ref[pl.ds(start, 8), :] * later
+
+    value = sol_ref[rows, :] - tree_sum([product(c) for c in range(8, 24)])
+    sol_ref[rows, :] = value - tree_sum([product(c) for c in range(8)])
+
+
+ENDS = 14
+LAST = 17
+
+
+def join_ends(mat_ref, rhs_ref, tmp_ref):
+    mine = lax.broadcasted_iota(jnp.int32, (8, LANES), 1) < 8
+    for first in range(ENDS, LAST):
+        for second in range(first, LAST):
+            u = second - first
+            for row in range(8):
+                start = (first * 8 + row) * WIN + 8 * u
+                value = jnp.where(mine, pltpu.roll(mat_ref[start:start + 8, :], LANES - 8, 1), 0.0)
+                tmp_ref[pl.ds(7 - row, 8, stride=9), :] = value
+            for row in range(8):
+                start = ((31 - second) * 8 + row) * WIN + 8 * u
+                mat_ref[start:start + 8, :] = mat_ref[start:start + 8, :] + tmp_ref[pl.ds((7 - row) * 9, 8), :]
+        value = jnp.where(mine, pltpu.roll(rhs_ref[first * 8:first * 8 + 8, :], LANES - 8, 1), 0.0)
+        for row in range(8):
+            tmp_ref[80 + 7 - row:80 + 8 - row, :] = value[row:row + 1]
+        start = (31 - first) * 8
+        rhs_ref[start:start + 8, :] = rhs_ref[start:start + 8, :] + tmp_ref[80:88, :]
+
+
+def spread_middle(sol_ref, tmp_ref):
     lane = lax.broadcasted_iota(jnp.int32, (8, LANES), 1)
+    for block in range(ENDS, LAST + 1):
+        value = pltpu.roll(sol_ref[block * 8:block * 8 + 8, :], 8, 1)
+        for row in range(8):
+            where = (LAST - block) * 8 + 7 - row
+            tmp_ref[where:where + 1, :] = value[row:row + 1]
+    for block in range(ENDS, LAST + 1):
+        other = tmp_ref[(block - ENDS) * 8:(block - ENDS) * 8 + 8, :]
+        rows = slice(block * 8, block * 8 + 8)
+        sol_ref[rows, :] = jnp.where(lane < 8, sol_ref[rows, :], other)
+
+
+def solve_kernel(phase_ref, offset_ref, out_ref, live_ref, mat_ref, rhs_ref, low_ref, back_ref, sol_ref, tmp_ref):
+    lane = lax.broadcasted_iota(jnp.int32, (8, LANES), 1)
+    backwards = LANES - 1 - lane
+
+    def flipped(value):
+        return jnp.take_along_axis(value, backwards, axis=1, mode="promise_in_bounds")
+
+    distance = SPAN - lax.broadcasted_iota(jnp.int32, (SPAN, LANES), 0)
+    for h in range(2):
+        hit = jnp.zeros((SPAN, LANES), F32)
+        for k in range(offset_ref.shape[0]):
+            entry = jnp.broadcast_to(offset_ref[k:k + 1, h * LANES:(h + 1) * LANES], (SPAN, LANES))
+            hit = jnp.where(entry == distance, 1.0, hit)
+        live_ref[h] = hit
     sol_ref[...] = jnp.zeros_like(sol_ref)
-    rhs_ref[...] = jnp.zeros_like(rhs_ref)
-    filler = jnp.zeros((LANES - 8, LANES), F32)
-
-    def turned(value):
-        return jnp.concatenate([value, filler], axis=0).T
+    blank = jnp.zeros((8, LANES), F32)
+
+    def turned(pairs):
+        rows = []
+        for low, high in pairs:
+            rows += [low, flipped(high)]
+        rows += [blank] * (16 - len(rows))
+        return jnp.concatenate(rows, axis=0).T
+
+    def current():
+        value = sol_ref[0:LANES, :].T
+        return [value[:8], flipped(value[8:16])]
+
+    def ahead(pair, shift):
+        a, b = (pltpu.roll(v, LANES - shift, 1) for v in pair)
+        keep = lane < LANES - shift
+        return [jnp.where(keep, a, b), jnp.where(keep, b, a)]
+
+    def behind(pair, shift):
+        a, b = (pltpu.roll(v, shift, 1) for v in pair)
+        keep = lane >= shift
+        return [jnp.where(keep, a, b), jnp.where(keep, b, a)]
 
     def round_body(_, carry):
-        now = [sol_ref[h * LANES:(h + 1) * LANES, :].T[:8] for h in range(2)]
+        now = current()
         degree = [jnp.full((8, LANES), ridge_weight, F32) for _ in range(2)]
         right = [jnp.zeros((8, LANES), F32) for _ in range(2)]
-
-        def clear(i, c):
-            mat_ref[pl.ds(pl.multiple_of(i * WIN + 24, 8), 8), :] = jnp.zeros((8, LANES), F32)
-            return c
-
-        lax.fori_loop(0, 256, clear, 0, unroll=8)
-
-        def ahead(pair, shift):
-            a, b = (pltpu.roll(v, LANES - shift, 1) for v in pair)
-            keep = lane < LANES - shift
-            return [jnp.where(keep, a, b), jnp.where(keep, b, a)]
-
-        def behind(pair, shift):
-            a, b = (pltpu.roll(v, shift, 1) for v in pair)
-            keep = lane >= shift
-            return [jnp.where(keep, a, b), jnp.where(keep, b, a)]
-
+        zero = jnp.zeros((8, LANES), F32)
+        for row in range(LANES):
+            mat_ref[row * WIN + 24:row * WIN + 32, :] = zero
+        for row in range(LANES, 144):
+            for t in range(4):
+                mat_ref[row * WIN + 8 * t:row * WIN + 8 * t + 8, :] = zero
+        rhs_ref[128:136, :] = zero
+        rhs_ref[136:144, :] = zero
+
+        stack = []
         for d in range(1, SPAN + 1):
             later = ahead(now, d)
             weights, moments = [], []
@@ -422,60 +484,65 @@
             for h in range(2):
                 degree[h] = degree[h] + (weights[h] + from_w[h])
                 right[h] = right[h] + (moments[h] - from_m[h])
-                column = turned(-weights[h])
-                for b in range(16):
-                    mat_ref[pl.ds((h * 16 + b) * 256 + d, 8, stride=WIN + 1), :] = column[b * 8:b * 8 + 8]
-        for h in range(2):
-            column = turned(degree[h])
-            for b in range(16):
-                mat_ref[pl.ds((h * 16 + b) * 256, 8, stride=WIN + 1), :] = column[b * 8:b * 8 + 8]
-            rhs_ref[h * LANES:(h + 1) * LANES, :] = turned(right[h])
+            crossing = jnp.where(lane < min(d, 16), 0.0, from_w[1])
+            stack.append((-weights[0], -crossing))
+            if len(stack) == 8:
+                columns = turned(stack)
+                for e in range(8):
+                    column = columns if e == 0 else pltpu.roll(columns, LANES - 16 * e, 1)
+                    for b in range(16):
+                        where = pl.ds(b * 256 + d - 7 + e, 8, stride=WIN + 1)
+                        mat_ref[where, :] = column[b * 8:b * 8 + 8]
+                stack = []
+        columns = turned([degree, right])
+        for b in range(16):
+            mat_ref[pl.ds(b * 256, 8, stride=WIN + 1), :] = columns[b * 8:b * 8 + 8]
+        rhs_ref[0:LANES, :] = pltpu.roll(columns, LANES - 16, 1)
 
         def forward(i, c):
-            factor_step(i, mat_ref, rhs_ref, low_ref, sol_ref)
+            factor_step(i, mat_ref, rhs_ref, low_ref, back_ref, sol_ref)
             return c
 
-        lax.fori_loop(0, 32, forward, 0)
-
-        def backward(i, c):
-            back_step(31 - i, mat_ref, sol_ref)
-            return c
-
-        lax.fori_loop(0, 32, backward, 0)
+        lax.fori_loop(0, ENDS, forward, 0)
+        join_ends(mat_ref, rhs_ref, tmp_ref)
+        lax.fori_loop(ENDS, LAST + 1, forward, 0)
+
+        for block in range(LAST, ENDS - 1, -1):
+            back_step(block, back_ref, sol_ref)
+        spread_middle(sol_ref, tmp_ref)
+        for block in range(ENDS - 1, -1, -1):
+            back_step(block, back_ref, sol_ref)
         return carry
 
     lax.fori_loop(0, ITERS, round_body, 0)
+    now = current()
     for h in range(2):
-        out_ref[:, h * LANES:(h + 1) * LANES] = sol_ref[h * LANES:(h + 1) * LANES, :].T[:8]
-
-
-def solve(phases, live):
+        out_ref[:, h * LANES:(h + 1) * LANES] = now[h]
+
+
+def solve(phases, offsets):
     return pl.pallas_call(
         solve_kernel,
         out_shape=jax.ShapeDtypeStruct((8, 256), F32),
         in_specs=[pl.BlockSpec(memory_space=pltpu.VMEM)] * 2,
         out_specs=pl.BlockSpec(memory_space=pltpu.VMEM),
         scratch_shapes=[
-            pltpu.VMEM((280 * WIN, LANES), F32),
-            pltpu.VMEM((280, LANES), F32),
+            pltpu.VMEM((2, SPAN, LANES), F32),
+            pltpu.VMEM((168 * WIN, LANES), F32),
+            pltpu.VMEM((168, LANES), F32),
             pltpu.VMEM((8 * 24, LANES), F32),
-            pltpu.VMEM((280, LANES), F32),
+            pltpu.VMEM((18 * 24 * 9, LANES), F32),
+            pltpu.VMEM((168, LANES), F32),
+            pltpu.VMEM((96, LANES), F32),
         ],
         name="solve",
-    )(phases, live)
-
-
-def live_mask(offsets):
-    distance = (SPAN - jnp.arange(WIN, dtype=jnp.int32))[:, None, None]
-    hit = jnp.any((offsets[None] == distance) & (offsets[None] > 0), axis=2)
-    return hit.astype(F32).reshape(WIN, 2, LANES).transpose(1, 0, 2)
+    )(phases, offsets)
 
 
 def local(slc, offsets):
-    live = live_mask(offsets)
     rows_first = jnp.transpose(slc, (0, 2, 1, 3))
     phases = pair_phases(rows_first, lax.axis_size("date"), lax.axis_size("tile"))
-    series = solve(phases, live)
+    series = solve(phases, offsets.T)
     return series.T[:, None, :]
 
 

time: 78.8 us -> 65 us (0.82)
  Pallas kernels: 77 us -> 64.9 us
  other arithmetic: 1.59 us -> 0 us
    pallas_call x1, Pallas kernels: 27.3 us -> 15.1 us  [solve(): pl.pallas_call(solve_kernel, out_shape=jax.ShapeDtypeStruct((8, 256), F32...]
    gt x1 -> x0, other arithmetic: 0.81 us -> none  [live_mask(): hit = jnp.any((offsets[None] == distance) & (offsets[None] > 0), axis=2)]
where the time goes in v3:
time: 65 us; the launch traced here: 64.9 us
  Pallas kernels  64.9 us (100%)
    pallas_call x1, Pallas kernels, pair_phases(): pl.pallas_call(front_kernel, out_shape=jax.ShapeDtypeStruct((2, 256, LANE...  49.8 us
    pallas_call x1, Pallas kernels, solve(): pl.pallas_call(solve_kernel, out_shape=jax.ShapeDtypeStruct((8, 256), F32...  15.1 us

profile of v3, /device:TPU:1, one launch (start us, length us, event | category | flops | bytes accessed | tf_op | source)
XLA Modules:
  0.0 64.9 jit_solution(1230306635083612299)
XLA Ops:
  0.0 49.8 %pair_phases.1.phase_ref = f32[2,256,128]{2,1,0:T(8,128)} custom-call(bf16[2,10,8,2560]{3,2,1,0:T(8,128)(2,1)} %bitcast.5), custom_call_target="tpu_custom_call" | custom-call | tf_op jit(solution)/shard_map/pair_phases/pallas_call | solution.py:270
  49.8 15.1 %solve.1 = f32[8,256]{1,0:T(8,128)} custom-call(f32[2,256,128]{2,1,0:T(8,128)} %pair_phases.1.phase_ref, s32[20,256]{1,0:T(8,128)} %bitcast.6), custom_call_target="tpu_custom_call" | custom-call | tf_op jit(solution)/shard_map/solve/pallas_call | solution.py:524

commit v4 on v3

--- a/solution.py
+++ b/solution.py
@@ -16,8 +16,11 @@
 ridge_weight = 1.0
 F32 = jnp.float32
 MESH = pl.DeviceIdType.MESH
-OWNERS = 6
+OWNERS = 12
 OWNER_STEP = 5
+OWNER_INVERSE = 13
+GROUPS = 1
+RING = 4
 
 
 def gather_step(step, slc_ref, send_ref):
@@ -72,31 +75,51 @@
     return pltpu.roll(value, shift, 1, stride=1, stride_axis=0)
 
 
-def front_kernel(slc_ref, phase_ref, send_ref, recv_ref, gram_ref, total_ref, band_ref, part_ref,
-                 gathered_ref, anchor_ref, send_sem, recv_sem, part_send, part_recv, column_send,
-                 column_recv, plane_send, plane_recv):
+def front_kernel(slc_hbm, phase_ref, slc_ref, send_ref, recv_ref, gram_ref, total_ref, band_ref,
+                 part_ref, gathered_ref, anchor_ref, load_sem, send_sem, recv_sem, part_send,
+                 part_recv, column_send, column_recv, plane_send, plane_recv):
     dates = send_ref.shape[0]
     tiles = lax.axis_size("tile")
     me = lax.axis_index("date")
     tile = lax.axis_index("tile")
     middle = tiles // 2
+    pixels = 8 // GROUPS
     lane = lax.broadcasted_iota(jnp.int32, (8, LANES), 1)
+    load = pltpu.make_async_copy(slc_hbm, slc_ref, load_sem)
+    load.start()
 
     def peer(k):
-        return lax.rem(me + k, dates)
+        return me ^ (dates - 1 - k)
+
+    def for_peers(action):
+        def go(k, carry):
+            action(peer(k))
+            return carry
+
+        lax.fori_loop(0, dates - 1, go, 0, unroll=True)
+
+    def for_far_peers(action):
+        steps = [(dx, dy, dc) for dx in range(RING) for dy in range(RING) for dc in range(2)]
+        steps.sort(key=lambda v: -(min(v[0], RING - v[0]) + min(v[1], RING - v[1]) + v[2] / 4))
+        for dx, dy, dc in steps[:-1]:
+            across = (me // (2 * RING) + dx) % RING
+            along = (me // 2 + dy) % RING
+            core = (me + dc) % 2
+            action((across * RING + along) * 2 + core)
+
+    def for_column(action):
+        def go(k, carry):
+            action(lax.rem(tile + k, tiles))
+            return carry
+
+        lax.fori_loop(1, tiles, go, 0)
 
     barrier = pltpu.get_barrier_semaphore()
-
-    def greet(k, carry):
-        pl.semaphore_signal(barrier, inc=1, device_id={"date": peer(k)}, device_id_type=MESH)
-        return carry
-
-    def greet_column(k, carry):
-        pl.semaphore_signal(barrier, inc=1, device_id={"tile": lax.rem(tile + k, tiles)}, device_id_type=MESH)
-        return carry
-
-    lax.fori_loop(1, dates, greet, 0)
-    lax.fori_loop(1, tiles, greet_column, 0)
+    for_column(lambda other: pl.semaphore_signal(
+        barrier, inc=1, device_id={"tile": other}, device_id_type=MESH))
+    for_peers(lambda other: pl.semaphore_signal(
+        barrier, inc=1, device_id={"date": other}, device_id_type=MESH))
+    load.wait()
 
     def gather(step, carry):
         gather_step(step, slc_ref, send_ref)
@@ -105,52 +128,60 @@
     lax.fori_loop(0, 8, gather, 0)
     pl.semaphore_wait(barrier, dates - 1 + tiles - 1)
 
-    def sample_copy(other, slot):
+    def sample_copy(group, other, slot):
+        part = pl.ds(group * pixels, pixels)
         return pltpu.make_async_remote_copy(
-            src_ref=send_ref.at[other], dst_ref=recv_ref.at[slot],
-            send_sem=send_sem.at[other], recv_sem=recv_sem.at[slot],
+            src_ref=send_ref.at[other, part], dst_ref=recv_ref.at[slot, part],
+            send_sem=send_sem.at[group, other], recv_sem=recv_sem.at[group, slot],
             device_id={"date": other}, device_id_type=MESH)
 
-    def send(k, carry):
-        sample_copy(peer(k), me).start()
-        return carry
-
-    lax.fori_loop(1, dates, send, 0)
+    for group in range(GROUPS):
+        for_far_peers(lambda other: sample_copy(group, other, me).start())
     recv_ref[me] = send_ref[me]
-
-    def arrive(k, carry):
-        other = peer(k)
-        sample_copy(other, other).wait_recv()
-        return carry
-
-    lax.fori_loop(1, dates, arrive, 0)
 
     row_id = lax.broadcasted_iota(jnp.int32, (256, 256), 0)
     col_id = lax.broadcasted_iota(jnp.int32, (256, 256), 1)
     mirror = (row_id + col_id == 255).astype(F32).astype(jnp.bfloat16)
     contract = (((1,), (1,)), ((), ()))
-    total_ref[...] = jnp.zeros_like(total_ref)
-
-    def grams(pixel, carry):
-        both = recv_ref[:, pixel].astype(F32)
-        real = both[:, :8].reshape(256, LANES)
-        imag = both[:, 8:].reshape(256, LANES)
-        right = jnp.concatenate([real, imag], axis=1).astype(jnp.bfloat16)
-        turned = jnp.concatenate([imag, -real], axis=1).astype(jnp.bfloat16)
-        descending = jnp.dot(mirror, right, preferred_element_type=F32).astype(jnp.bfloat16)
-        for part, left in enumerate((right, turned)):
-            gram = lax.dot_general(left, descending, contract, preferred_element_type=F32)
-            gram_ref[pixel, part] = gram
-            total_ref[part] = total_ref[part] + gram
-        return carry
-
-    lax.fori_loop(0, 8, grams, 0)
+
+    for group in range(GROUPS):
+        for_peers(lambda other: sample_copy(group, other, other).wait_recv())
+        total = [None, None]
+        for pixel in range(group * pixels, (group + 1) * pixels):
+            both = recv_ref[:, pixel].astype(F32)
+            real = both[:, :8].reshape(256, LANES)
+            imag = both[:, 8:].reshape(256, LANES)
+            right = jnp.concatenate([real, imag], axis=1).astype(jnp.bfloat16)
+            turned = jnp.concatenate([imag, -real], axis=1).astype(jnp.bfloat16)
+            descending = jnp.dot(mirror, right, preferred_element_type=F32).astype(jnp.bfloat16)
+            for part, left in enumerate((right, turned)):
+                gram = lax.dot_general(left, descending, contract, preferred_element_type=F32)
+                gram_ref[pixel, part] = gram
+                if pixel == 0:
+                    total_ref[part] = gram
+                else:
+                    total_ref[part] = total_ref[part] + gram
+
+    def owner_date(owner):
+        return lax.rem(owner * OWNER_STEP, dates)
+
+    owned = lax.rem(me * OWNER_INVERSE, dates)
 
     def part_copy(owner, slot):
         return pltpu.make_async_remote_copy(
             src_ref=part_ref.at[owner], dst_ref=gathered_ref.at[slot],
             send_sem=part_send.at[owner], recv_sem=part_recv.at[slot],
-            device_id={"date": owner * OWNER_STEP}, device_id_type=MESH)
+            device_id={"date": owner_date(owner)}, device_id_type=MESH)
+
+    def for_owners(action):
+        def go(owner, carry):
+            @pl.when(owner != owned)
+            def _():
+                action(owner)
+
+            return carry
+
+        lax.fori_loop(0, OWNERS, go, 0, unroll=True)
 
     @pl.when(tile == middle)
     def _():
@@ -159,14 +190,11 @@
             band_ref[0, 0, block * 8:block * 8 + 8, :] = value
         for half in range(2):
             turned = band_ref[0, 0, half * LANES:(half + 1) * LANES, :].T
-            for third in range(3):
-                owner = half * 3 + third
-                part_ref[owner, 0:8, :] = turned[third * 8:third * 8 + 8]
-                part_ref[owner, 8:16, :] = turned[WIN + third * 8:WIN + third * 8 + 8]
-        for owner in range(OWNERS):
-            @pl.when(me != owner * OWNER_STEP)
-            def _():
-                part_copy(owner, me).start()
+            for sixth in range(6):
+                owner = half * 6 + sixth
+                part_ref[owner, 0:4, :] = turned[sixth * 4:sixth * 4 + 4]
+                part_ref[owner, 4:8, :] = turned[WIN + sixth * 4:WIN + sixth * 4 + 4]
+        for_owners(lambda owner: part_copy(owner, me).start())
 
     def bands(group, carry):
         for part in range(2):
@@ -197,97 +225,73 @@
             send_sem=plane_send.at[other], recv_sem=plane_recv.at[owner],
             device_id={"date": other}, device_id_type=MESH)
 
-    def plane_start(owner):
-        def go(k, carry):
-            plane_copy(owner, peer(k)).start()
-            return carry
-
-        lax.fori_loop(1, dates, go, 0)
-
-    for owner in range(OWNERS):
-        @pl.when((me == owner * OWNER_STEP) & (tile == middle))
-        def _():
-            def part_arrive(k, total):
-                other = peer(k)
-                part_copy(owner, other).wait_recv()
-                return total + gathered_ref[other]
-
-            total = lax.fori_loop(1, dates, part_arrive, part_ref[owner])
-            anchor_ref[owner] = jnp.arctan2(total[8:], total[:8])
-
-            def go(k, carry):
-                column_copy(owner, lax.rem(tile + k, tiles)).start()
-                return carry
-
-            lax.fori_loop(1, tiles, go, 0)
-            plane_start(owner)
-
-        @pl.when((me == owner * OWNER_STEP) & (tile != middle))
-        def _():
-            column_copy(owner, middle).wait_recv()
-            plane_start(owner)
-
-    for owner in range(OWNERS):
-        @pl.when(me != owner * OWNER_STEP)
-        def _():
-            plane_copy(owner, owner * OWNER_STEP).wait_recv()
+    @pl.when((owned < OWNERS) & (tile == middle))
+    def _():
+        def part_arrive(k, total):
+            other = peer(k)
+            part_copy(owned, other).wait_recv()
+            return total + gathered_ref[other]
+
+        total = lax.fori_loop(0, dates - 1, part_arrive, part_ref[owned])
+        anchor_ref[owned] = jnp.arctan2(total[4:], total[:4])
+        for_column(lambda other: column_copy(owned, other).start())
+
+    @pl.when((owned < OWNERS) & (tile != middle))
+    def _():
+        column_copy(owned, middle).wait_recv()
+
+    @pl.when(owned < OWNERS)
+    def _():
+        for_far_peers(lambda other: plane_copy(owned, other).start())
+
+    for group in range(GROUPS):
+        for_peers(lambda other: sample_copy(group, other, me).wait_send())
+
+    @pl.when(tile == middle)
+    def _():
+        for_owners(lambda owner: part_copy(owner, me).wait_send())
+
+    for_owners(lambda owner: plane_copy(owner, owner_date(owner)).wait_recv())
 
     for half in range(2):
-        base = jnp.concatenate([anchor_ref[half * 3 + t] for t in range(3)], axis=0)
+        base = jnp.concatenate([anchor_ref[half * 6 + t] for t in range(6)], axis=0)
         for pixel in range(8):
             rows = slice(pixel * WIN, pixel * WIN + SPAN)
             phase_ref[half, rows, :] = phase_ref[half, rows, :] - base
 
-    def drain(k, carry):
-        sample_copy(peer(k), me).wait_send()
-        return carry
-
-    lax.fori_loop(1, dates, drain, 0)
-    for owner in range(OWNERS):
-        @pl.when((me != owner * OWNER_STEP) & (tile == middle))
-        def _():
-            part_copy(owner, me).wait_send()
-
-        @pl.when(me == owner * OWNER_STEP)
-        def _():
-            def done(k, carry):
-                plane_copy(owner, peer(k)).wait_send()
-                return carry
-
-            lax.fori_loop(1, dates, done, 0)
-
-        @pl.when((me == owner * OWNER_STEP) & (tile == middle))
-        def _():
-            def done(k, carry):
-                column_copy(owner, lax.rem(tile + k, tiles)).wait_send()
-                return carry
-
-            lax.fori_loop(1, tiles, done, 0)
+    @pl.when(owned < OWNERS)
+    def _():
+        for_peers(lambda other: plane_copy(owned, other).wait_send())
+
+    @pl.when((owned < OWNERS) & (tile == middle))
+    def _():
+        for_column(lambda other: column_copy(owned, other).wait_send())
 
 
 def pair_phases(slc, dates, tiles):
-    groups = dates
     return pl.pallas_call(
         front_kernel,
         out_shape=jax.ShapeDtypeStruct((2, 256, LANES), F32),
-        in_specs=[pl.BlockSpec(memory_space=pltpu.VMEM)],
+        in_specs=[pl.BlockSpec(memory_space=pl.ANY)],
         out_specs=pl.BlockSpec(memory_space=pltpu.VMEM),
         scratch_shapes=[
-            pltpu.VMEM((groups, 8, 16, LANES), jnp.bfloat16),
-            pltpu.VMEM((groups, 8, 16, LANES), jnp.bfloat16),
+            pltpu.VMEM(slc.shape, slc.dtype),
+            pltpu.VMEM((dates, 8, 16, LANES), jnp.bfloat16),
+            pltpu.VMEM((dates, 8, 16, LANES), jnp.bfloat16),
             pltpu.VMEM((8, 2, 256, 256), F32),
             pltpu.VMEM((2, 256, 256), F32),
             pltpu.VMEM((2, 2, 256, LANES), F32),
-            pltpu.VMEM((OWNERS, 16, LANES), F32),
-            pltpu.VMEM((groups, 16, LANES), F32),
             pltpu.VMEM((OWNERS, 8, LANES), F32),
-            pltpu.SemaphoreType.DMA((groups,)),
-            pltpu.SemaphoreType.DMA((groups,)),
+            pltpu.VMEM((dates, 8, LANES), F32),
+            pltpu.VMEM((OWNERS, 4, LANES), F32),
+            pltpu.SemaphoreType.DMA(()),
+            pltpu.SemaphoreType.DMA((GROUPS, dates)),
+            pltpu.SemaphoreType.DMA((GROUPS, dates)),
             pltpu.SemaphoreType.DMA((OWNERS,)),
-            pltpu.SemaphoreType.DMA((groups,)),
+            pltpu.SemaphoreType.DMA((dates,)),
             pltpu.SemaphoreType.DMA((tiles,)),
             pltpu.SemaphoreType.DMA((1,)),
-            pltpu.SemaphoreType.DMA((groups,)),
+            pltpu.SemaphoreType.DMA((dates,)),
             pltpu.SemaphoreType.DMA((OWNERS,)),
         ],
         compiler_params=pltpu.CompilerParams(collective_id=0, has_side_effects=True),

time: 65 us -> 58.4 us (0.90)
  Pallas kernels: 64.9 us -> 58.2 us
    pallas_call x1, Pallas kernels: 49.8 us -> 43.1 us  [pair_phases(): pl.pallas_call(front_kernel, out_shape=jax.ShapeDtypeStruct((2, 256, LANE...]
where the time goes in v4:
time: 58.4 us; the launch traced here: 58.2 us
  Pallas kernels  58.2 us (100%)
    pallas_call x1, Pallas kernels, pair_phases(): pl.pallas_call(front_kernel, out_shape=jax.ShapeDtypeStruct((2, 256, LANE...  43.1 us
    pallas_call x1, Pallas kernels, solve(): pl.pallas_call(solve_kernel, out_shape=jax.ShapeDtypeStruct((8, 256), F32...  15.1 us

profile of v4, /device:TPU:1, one launch (start us, length us, event | category | flops | bytes accessed | tf_op | source)
XLA Modules:
  0.0 58.2 jit_solution(17169960432031779182)
XLA Ops:
  0.0 43.1 %pair_phases.1.phase_ref = f32[2,256,128]{2,1,0:T(8,128)} custom-call(bf16[2,10,8,2560]{3,2,1,0:T(8,128)(2,1)} %bitcast.5), custom_call_target="tpu_custom_call" | custom-call | tf_op jit(solution)/shard_map/pair_phases/pallas_call | solution.py:272
  43.1 15.1 %solve.1 = f32[8,256]{1,0:T(8,128)} custom-call(f32[2,256,128]{2,1,0:T(8,128)} %pair_phases.1.phase_ref, s32[20,256]{1,0:T(8,128)} %bitcast.6), custom_call_target="tpu_custom_call" | custom-call | tf_op jit(solution)/shard_map/solve/pallas_call | solution.py:528

commit v5 on v4

--- a/solution.py
+++ b/solution.py
@@ -19,7 +19,6 @@
 OWNERS = 12
 OWNER_STEP = 5
 OWNER_INVERSE = 13
-GROUPS = 1
 RING = 4
 
 
@@ -83,7 +82,6 @@
     me = lax.axis_index("date")
     tile = lax.axis_index("tile")
     middle = tiles // 2
-    pixels = 8 // GROUPS
     lane = lax.broadcasted_iota(jnp.int32, (8, LANES), 1)
     load = pltpu.make_async_copy(slc_hbm, slc_ref, load_sem)
     load.start()
@@ -121,22 +119,19 @@
         barrier, inc=1, device_id={"date": other}, device_id_type=MESH))
     load.wait()
 
+    def sample_copy(other, slot):
+        return pltpu.make_async_remote_copy(
+            src_ref=send_ref.at[other], dst_ref=recv_ref.at[slot],
+            send_sem=send_sem.at[other], recv_sem=recv_sem.at[slot],
+            device_id={"date": other}, device_id_type=MESH)
+
     def gather(step, carry):
         gather_step(step, slc_ref, send_ref)
         return carry
 
     lax.fori_loop(0, 8, gather, 0)
     pl.semaphore_wait(barrier, dates - 1 + tiles - 1)
-
-    def sample_copy(group, other, slot):
-        part = pl.ds(group * pixels, pixels)
-        return pltpu.make_async_remote_copy(
-            src_ref=send_ref.at[other, part], dst_ref=recv_ref.at[slot, part],
-            send_sem=send_sem.at[group, other], recv_sem=recv_sem.at[group, slot],
-            device_id={"date": other}, device_id_type=MESH)
-
-    for group in range(GROUPS):
-        for_far_peers(lambda other: sample_copy(group, other, me).start())
+    for_far_peers(lambda other: sample_copy(other, me).start())
     recv_ref[me] = send_ref[me]
 
     row_id = lax.broadcasted_iota(jnp.int32, (256, 256), 0)
@@ -144,23 +139,21 @@
     mirror = (row_id + col_id == 255).astype(F32).astype(jnp.bfloat16)
     contract = (((1,), (1,)), ((), ()))
 
-    for group in range(GROUPS):
-        for_peers(lambda other: sample_copy(group, other, other).wait_recv())
-        total = [None, None]
-        for pixel in range(group * pixels, (group + 1) * pixels):
-            both = recv_ref[:, pixel].astype(F32)
-            real = both[:, :8].reshape(256, LANES)
-            imag = both[:, 8:].reshape(256, LANES)
-            right = jnp.concatenate([real, imag], axis=1).astype(jnp.bfloat16)
-            turned = jnp.concatenate([imag, -real], axis=1).astype(jnp.bfloat16)
-            descending = jnp.dot(mirror, right, preferred_element_type=F32).astype(jnp.bfloat16)
-            for part, left in enumerate((right, turned)):
-                gram = lax.dot_general(left, descending, contract, preferred_element_type=F32)
-                gram_ref[pixel, part] = gram
-                if pixel == 0:
-                    total_ref[part] = gram
-                else:
-                    total_ref[part] = total_ref[part] + gram
+    for_peers(lambda other: sample_copy(other, other).wait_recv())
+    for pixel in range(8):
+        both = recv_ref[:, pixel].astype(F32)
+        real = both[:, :8].reshape(256, LANES)
+        imag = both[:, 8:].reshape(256, LANES)
+        right = jnp.concatenate([real, imag], axis=1).astype(jnp.bfloat16)
+        turned = jnp.concatenate([imag, -real], axis=1).astype(jnp.bfloat16)
+        descending = jnp.dot(mirror, right, preferred_element_type=F32).astype(jnp.bfloat16)
+        for part, left in enumerate((right, turned)):
+            gram = lax.dot_general(left, descending, contract, preferred_element_type=F32)
+            gram_ref[pixel, part] = gram
+            if pixel == 0:
+                total_ref[part] = gram
+            else:
+                total_ref[part] = total_ref[part] + gram
 
     def owner_date(owner):
         return lax.rem(owner * OWNER_STEP, dates)
@@ -244,8 +237,7 @@
     def _():
         for_far_peers(lambda other: plane_copy(owned, other).start())
 
-    for group in range(GROUPS):
-        for_peers(lambda other: sample_copy(group, other, me).wait_send())
+    for_peers(lambda other: sample_copy(other, me).wait_send())
 
     @pl.when(tile == middle)
     def _():
@@ -285,8 +277,8 @@
             pltpu.VMEM((dates, 8, LANES), F32),
             pltpu.VMEM((OWNERS, 4, LANES), F32),
             pltpu.SemaphoreType.DMA(()),
-            pltpu.SemaphoreType.DMA((GROUPS, dates)),
-            pltpu.SemaphoreType.DMA((GROUPS, dates)),
+            pltpu.SemaphoreType.DMA((dates,)),
+            pltpu.SemaphoreType.DMA((dates,)),
             pltpu.SemaphoreType.DMA((OWNERS,)),
             pltpu.SemaphoreType.DMA((dates,)),
             pltpu.SemaphoreType.DMA((tiles,)),
@@ -299,8 +291,12 @@
     )(slc)
 
 
-def factor_step(block, mat_ref, rhs_ref, low_ref, back_ref, sol_ref):
-    base = pl.multiple_of(block * 256, 256)
+def aligned(value, unit):
+    return value if isinstance(value, int) else pl.multiple_of(value, unit)
+
+
+def factor_step(block, mat_ref, rhs_ref, low_ref, back_ref, sol_ref, tiles=3):
+    base = aligned(block * 256, 256)
 
     def spread(ref, row):
         return jnp.broadcast_to(ref[pl.ds(row, 1), :], (8, LANES))
@@ -311,8 +307,8 @@
             s[i, j] = spread(mat_ref, base + i * WIN + j)
     rows = []
     for i in range(8):
-        tiles = [mat_ref[pl.ds(pl.multiple_of(base + i * WIN + 8 * t, 8), 8), :] for t in (1, 2, 3)]
-        rows.append(tiles + [spread(rhs_ref, block * 8 + i)])
+        later = [mat_ref[pl.ds(aligned(base + i * WIN + 8 * t, 8), 8), :] for t in range(1, tiles + 1)]
+        rows.append(later + [spread(rhs_ref, block * 8 + i)])
     mult = {}
     inverse = []
     for a in (0, 2, 4, 6):
@@ -328,42 +324,44 @@
             for j in range(i, 8):
                 s[i, j] = s[i, j] - mult[i, a] * s[a, j] - mult[i, b] * s[b, j]
         for i in range(a + 2, 8):
-            rows[i] = [rows[i][t] - mult[i, a] * rows[a][t] - mult[i, b] * rows[b][t] for t in range(4)]
+            rows[i] = [rows[i][t] - mult[i, a] * rows[a][t] - mult[i, b] * rows[b][t] for t in range(tiles + 1)]
     scaled = [None] * 8
     for index, a in enumerate((0, 2, 4, 6)):
         e11, e12, e22 = inverse[index]
-        scaled[a] = [e11 * rows[a][t] + e12 * rows[a + 1][t] for t in range(4)]
-        scaled[a + 1] = [e12 * rows[a][t] + e22 * rows[a + 1][t] for t in range(4)]
+        scaled[a] = [e11 * rows[a][t] + e12 * rows[a + 1][t] for t in range(tiles + 1)]
+        scaled[a + 1] = [e12 * rows[a][t] + e22 * rows[a + 1][t] for t in range(tiles + 1)]
     for k in range(8):
-        for t in range(3):
+        for t in range(tiles):
             low_ref[k * 24 + 8 * t:k * 24 + 8 * t + 8, :] = scaled[k][t]
-    for r in range(24):
+    for r in range(8 * tiles):
         t = r // 8
-        target = pl.multiple_of((block + 1) * 256, 256) + r * WIN
-        factors = [jnp.broadcast_to(low_ref[k * 24 + r:k * 24 + r + 1, :], (8, LANES)) for k in range(8)]
-        for u in range(t, 3):
-            where = pl.ds(pl.multiple_of(target + (u - t) * 8, 8), 8)
+        target = aligned((block + 1) * 256, 256) + r * WIN
+        first = max(r - 16, 0) // 2 * 2
+        factors = {k: jnp.broadcast_to(low_ref[k * 24 + r:k * 24 + r + 1, :], (8, LANES))
+                   for k in range(first, 8)}
+        for u in range(t, tiles):
+            where = pl.ds(aligned(target + (u - t) * 8, 8), 8)
             value = mat_ref[where, :]
-            for k in range(8):
+            for k in range(first, 8):
                 value = value - factors[k] * rows[k][u]
             mat_ref[where, :] = value
-    for u in range(3):
-        where = pl.ds(pl.multiple_of((block + 1 + u) * 8, 8), 8)
+    for u in range(tiles):
+        where = pl.ds(aligned((block + 1 + u) * 8, 8), 8)
         value = rhs_ref[where, :]
         for k in range(8):
-            value = value - scaled[k][3] * rows[k][u]
+            value = value - scaled[k][tiles] * rows[k][u]
         rhs_ref[where, :] = value
     for a in (6, 4, 2, 0):
         for c in (a, a + 1):
             for i in range(a + 2, 8):
-                scaled[c] = [scaled[c][t] - mult[i, c] * scaled[i][t] for t in range(4)]
+                scaled[c] = [scaled[c][t] - mult[i, c] * scaled[i][t] for t in range(tiles + 1)]
     sub = lax.broadcasted_iota(jnp.int32, (8, LANES), 0)
-    answer = scaled[0][3]
+    answer = scaled[0][tiles]
     for i in range(1, 8):
-        answer = jnp.where(sub == i, scaled[i][3], answer)
-    sol_ref[pl.ds(pl.multiple_of(block * 8, 8), 8), :] = answer
+        answer = jnp.where(sub == i, scaled[i][tiles], answer)
+    sol_ref[pl.ds(aligned(block * 8, 8), 8), :] = answer
     for i in range(8):
-        for t in range(3):
+        for t in range(tiles):
             back_ref[pl.ds((block * 24 + 8 * t) * 9 + i, 8, stride=9), :] = scaled[i][t]
 
 
@@ -374,7 +372,7 @@
     return parts[0]
 
 
-def back_step(block, back_ref, sol_ref):
+def back_step(block, back_ref, sol_ref, tiles=3):
     rows = slice(block * 8, block * 8 + 8)
 
     def product(c):
@@ -382,8 +380,11 @@
         later = jnp.broadcast_to(sol_ref[block * 8 + 8 + c:block * 8 + 9 + c, :], (8, LANES))
         return back_ref[pl.ds(start, 8), :] * later
 
-    value = sol_ref[rows, :] - tree_sum([product(c) for c in range(8, 24)])
-    sol_ref[rows, :] = value - tree_sum([product(c) for c in range(8)])
+    value = sol_ref[rows, :]
+    if tiles > 1:
+        value = value - tree_sum([product(c) for c in range(8, 8 * tiles)])
+    if tiles > 0:
+        sol_ref[rows, :] = value - tree_sum([product(c) for c in range(8)])
 
 
 ENDS = 14
@@ -507,12 +508,13 @@
             factor_step(i, mat_ref, rhs_ref, low_ref, back_ref, sol_ref)
             return c
 
-        lax.fori_loop(0, ENDS, forward, 0)
+        lax.fori_loop(0, ENDS, forward, 0, unroll=2)
         join_ends(mat_ref, rhs_ref, tmp_ref)
-        lax.fori_loop(ENDS, LAST + 1, forward, 0)
+        for block in range(ENDS, LAST + 1):
+            factor_step(block, mat_ref, rhs_ref, low_ref, back_ref, sol_ref, LAST - block)
 
         for block in range(LAST, ENDS - 1, -1):
-            back_step(block, back_ref, sol_ref)
+            back_step(block, back_ref, sol_ref, LAST - block)
         spread_middle(sol_ref, tmp_ref)
         for block in range(ENDS - 1, -1, -1):
             back_step(block, back_ref, sol_ref)

time: 58.4 us -> 56.8 us (0.973)
  Pallas kernels: 58.2 us -> 56.7 us
    pallas_call x1, Pallas kernels: 15.1 us -> 13.6 us  [solve(): pl.pallas_call(solve_kernel, out_shape=jax.ShapeDtypeStruct((8, 256), F32...]
where the time goes in v5:
time: 56.8 us; the launch traced here: 56.7 us
  Pallas kernels  56.7 us (100%)
    pallas_call x1, Pallas kernels, pair_phases(): pl.pallas_call(front_kernel, out_shape=jax.ShapeDtypeStruct((2, 256, LANE...  43.1 us
    pallas_call x1, Pallas kernels, solve(): pl.pallas_call(solve_kernel, out_shape=jax.ShapeDtypeStruct((8, 256), F32...  13.6 us

profile of v5, /device:TPU:1, one launch (start us, length us, event | category | flops | bytes accessed | tf_op | source)
XLA Modules:
  0.0 56.7 jit_solution(15579318604790974441)
XLA Ops:
  0.0 43.1 %pair_phases.1.phase_ref = f32[2,256,128]{2,1,0:T(8,128)} custom-call(bf16[2,10,8,2560]{3,2,1,0:T(8,128)(2,1)} %bitcast.5), custom_call_target="tpu_custom_call" | custom-call | tf_op jit(solution)/shard_map/pair_phases/pallas_call | solution.py:264
  43.1 13.6 %solve.1 = f32[8,256]{1,0:T(8,128)} custom-call(f32[2,256,128]{2,1,0:T(8,128)} %pair_phases.1.phase_ref, s32[20,256]{1,0:T(8,128)} %bitcast.6), custom_call_target="tpu_custom_call" | custom-call | tf_op jit(solution)/shard_map/solve/pallas_call | solution.py:530

commit v6 on v5

--- a/solution.py
+++ b/solution.py
@@ -461,8 +461,8 @@
         keep = lane >= shift
         return [jnp.where(keep, a, b), jnp.where(keep, b, a)]
 
-    def round_body(_, carry):
-        now = current()
+    def one_round(first):
+        now = [blank, blank] if first else current()
         degree = [jnp.full((8, LANES), ridge_weight, F32) for _ in range(2)]
         right = [jnp.zeros((8, LANES), F32) for _ in range(2)]
         zero = jnp.zeros((8, LANES), F32)
@@ -476,11 +476,11 @@
 
         stack = []
         for d in range(1, SPAN + 1):
-            later = ahead(now, d)
+            later = now if first else ahead(now, d)
             weights, moments = [], []
             for h in range(2):
                 phase = phase_ref[h, pl.ds(SPAN - d, 8, stride=WIN), :]
-                residual = phase - (now[h] - later[h])
+                residual = phase if first else phase - (now[h] - later[h])
                 live = jnp.broadcast_to(live_ref[h, SPAN - d:SPAN - d + 1, :], (8, LANES))
                 weight = live / jnp.maximum(jnp.abs(residual), floor_value)
                 weights.append(weight)
@@ -518,9 +518,9 @@
         spread_middle(sol_ref, tmp_ref)
         for block in range(ENDS - 1, -1, -1):
             back_step(block, back_ref, sol_ref)
-        return carry
-
-    lax.fori_loop(0, ITERS, round_body, 0)
+
+    for number in range(ITERS):
+        one_round(number == 0)
     now = current()
     for h in range(2):
         out_ref[:, h * LANES:(h + 1) * LANES] = now[h]

time: 56.8 us -> 55.7 us (0.981)
  Pallas kernels: 56.7 us -> 55.6 us
    pallas_call x1, Pallas kernels: 13.6 us -> 12.4 us  [solve(): pl.pallas_call(solve_kernel, out_shape=jax.ShapeDtypeStruct((8, 256), F32...]
where the time goes in v6:
time: 55.7 us; the launch traced here: 55.6 us
  Pallas kernels  55.6 us (100%)
    pallas_call x1, Pallas kernels, pair_phases(): pl.pallas_call(front_kernel, out_shape=jax.ShapeDtypeStruct((2, 256, LANE...  43.1 us
    pallas_call x1, Pallas kernels, solve(): pl.pallas_call(solve_kernel, out_shape=jax.ShapeDtypeStruct((8, 256), F32...  12.4 us

profile of v6, /device:TPU:1, one launch (start us, length us, event | category | flops | bytes accessed | tf_op | source)
XLA Modules:
  0.0 55.6 jit_solution(8138349124397657471)
XLA Ops:
  0.0 43.1 %pair_phases.1.phase_ref = f32[2,256,128]{2,1,0:T(8,128)} custom-call(bf16[2,10,8,2560]{3,2,1,0:T(8,128)(2,1)} %bitcast.5), custom_call_target="tpu_custom_call" | custom-call | tf_op jit(solution)/shard_map/pair_phases/pallas_call | solution.py:264
  43.1 12.4 %solve.1 = f32[8,256]{1,0:T(8,128)} custom-call(f32[2,256,128]{2,1,0:T(8,128)} %pair_phases.1.phase_ref, s32[20,256]{1,0:T(8,128)} %bitcast.6), custom_call_target="tpu_custom_call" | custom-call | tf_op jit(solution)/shard_map/solve/pallas_call | solution.py:530

commit v7 on v6

--- a/solution.py
+++ b/solution.py
@@ -129,7 +129,7 @@
         gather_step(step, slc_ref, send_ref)
         return carry
 
-    lax.fori_loop(0, 8, gather, 0)
+    lax.fori_loop(0, 8, gather, 0, unroll=2)
     pl.semaphore_wait(barrier, dates - 1 + tiles - 1)
     for_far_peers(lambda other: sample_copy(other, me).start())
     recv_ref[me] = send_ref[me]

time: 55.7 us -> 55.7 us (level)
  no operation moved by 1% of the time
where the time goes in v7:
time: 55.7 us; the launch traced here: 55.6 us
  Pallas kernels  55.6 us (100%)
    pallas_call x1, Pallas kernels, pair_phases(): pl.pallas_call(front_kernel, out_shape=jax.ShapeDtypeStruct((2, 256, LANE...  43.1 us
    pallas_call x1, Pallas kernels, solve(): pl.pallas_call(solve_kernel, out_shape=jax.ShapeDtypeStruct((8, 256), F32...  12.4 us

profile of v7, /device:TPU:1, one launch (start us, length us, event | category | flops | bytes accessed | tf_op | source)
XLA Modules:
  0.0 55.6 jit_solution(16160258927922881764)
XLA Ops:
  0.0 43.1 %pair_phases.1.phase_ref = f32[2,256,128]{2,1,0:T(8,128)} custom-call(bf16[2,10,8,2560]{3,2,1,0:T(8,128)(2,1)} %bitcast.5), custom_call_target="tpu_custom_call" | custom-call | tf_op jit(solution)/shard_map/pair_phases/pallas_call | solution.py:264
  43.1 12.4 %solve.1 = f32[8,256]{1,0:T(8,128)} custom-call(f32[2,256,128]{2,1,0:T(8,128)} %pair_phases.1.phase_ref, s32[20,256]{1,0:T(8,128)} %bitcast.6), custom_call_target="tpu_custom_call" | custom-call | tf_op jit(solution)/shard_map/solve/pallas_call | solution.py:530
